TPU v7x, 32 devices: a whole 2x2x4 slice. The times are simulated.
32 devices in a mesh: chain: 4 (over y, x), op: 8 (over z, core).
Axes of the slice: x: 2, y: 2, z: 4, core: 2. Of those that a mesh axis runs over, the one named last changes fastest.
Arguments:
- env_in: bfloat16 [16, 16, 128, 128], P('op'), may hold values from -6 to 6
- mps: bfloat16 [4, 4, 16, 128, 128], P('chain'), may hold values from -0.5 to 0.5
- proj: bfloat16 [4, 4, 16, 128, 128], P('chain'), may hold values from -0.5 to 0.5
- mpo: bfloat16 [4, 16, 4, 16, 4], P('chain'), may hold values from -2 to 2
- mpo_charge: int32 [16, 2], replicated, may hold values from -1 to 1
- block_sizes: int32 [5, 16], replicated, may hold values from 32 to 128
Outputs:
- env_out: bfloat16 [4, 16, 16, 128, 128], P('chain', 'op')
All inputs are finite; a program needn't handle non-finite values.
Results may differ from a plain program's by a relative error of at most 0.025.
Values may be sent and summed in bfloat16 or wider, within the bound.
No kernel may reach another device: no remote copies, remote signals or barrier semaphores. Data moves between devices by JAX's collectives and lax.ppermute only.
A program may use at most 64 MiB of HBM per device.

v0:
```python
import jax
import jax.numpy as jnp
from jax import lax
from jax.sharding import PartitionSpec as P

MPO_BOND = 16
BLOCK_DIM = 128
UP_VALUES = 8
DOWN_VALUES = 2
SECTORS = 16


UP_CHARGE = (0, 1, 0, 1)
DOWN_CHARGE = (0, 0, 1, 1)


def from_behind(block, axis, distance):
    devices = range(lax.axis_size(axis))
    route = [(i - distance, i) for i in devices if i - distance in devices]
    return lax.ppermute(block, axis, route)


def mask_site(site_mps, site_proj, left_sizes, right_sizes):
    positions = jnp.arange(BLOCK_DIM, dtype=jnp.int32)
    up_index = jnp.arange(UP_VALUES, dtype=jnp.int32)[:, None]
    down_index = jnp.arange(DOWN_VALUES, dtype=jnp.int32)[None, :]
    left_grid = left_sizes.reshape(UP_VALUES, DOWN_VALUES)
    right_grid = jnp.pad(right_sizes.reshape(UP_VALUES, DOWN_VALUES), ((0, 1), (0, 1)))
    mps_grid = site_mps.reshape(4, UP_VALUES, DOWN_VALUES, BLOCK_DIM, BLOCK_DIM)
    proj_grid = site_proj.reshape(4, UP_VALUES, DOWN_VALUES, BLOCK_DIM, BLOCK_DIM)
    mps_parts = []
    proj_parts = []
    for phys_state in range(4):
        up_shift = UP_CHARGE[phys_state]
        down_shift = DOWN_CHARGE[phys_state]
        right_here = right_grid[
            up_shift : up_shift + UP_VALUES, down_shift : down_shift + DOWN_VALUES
        ]
        row_keep = positions[None, None, :] < left_grid[:, :, None]
        column_keep = positions[None, None, :] < right_here[:, :, None]
        keep_mask = row_keep[:, :, :, None] & column_keep[:, :, None, :]
        mps_parts.append(
            jnp.where(keep_mask, mps_grid[phys_state], jnp.zeros_like(mps_grid[phys_state]))
        )
        inside = (up_index + up_shift < UP_VALUES) & (down_index + down_shift < DOWN_VALUES)
        proj_parts.append(
            jnp.where(
                inside[:, :, None, None],
                proj_grid[phys_state],
                jnp.zeros_like(proj_grid[phys_state]),
            )
        )
    return (jnp.stack(mps_parts, axis=0), jnp.stack(proj_parts, axis=0))


def mask_mpo(site_mpo, mpo_charge):
    up_state = jnp.array(UP_CHARGE, dtype=jnp.int32)
    down_state = jnp.array(DOWN_CHARGE, dtype=jnp.int32)
    up_bond = mpo_charge[:, 0]
    down_bond = mpo_charge[:, 1]
    match_up = (
        up_bond[:, None, None, None] + up_state[None, None, None, :]
        == up_state[None, :, None, None] + up_bond[None, None, :, None]
    )
    match_down = (
        down_bond[:, None, None, None] + down_state[None, None, None, :]
        == down_state[None, :, None, None] + down_bond[None, None, :, None]
    )
    return jnp.where(match_up & match_down, site_mpo, jnp.zeros_like(site_mpo))


def mix_row(current, previous, mps_grid, row_index):
    pieces = []
    for phys_state in range(4):
        up_shift = UP_CHARGE[phys_state]
        down_shift = DOWN_CHARGE[phys_state]
        env_row = previous if up_shift else current
        source_row = row_index - up_shift
        mps_row = lax.dynamic_index_in_dim(
            mps_grid[phys_state], jnp.maximum(source_row, 0), 0, keepdims=False
        )
        mps_row = jnp.where(source_row >= 0, mps_row, jnp.zeros_like(mps_row))
        if down_shift:
            env_row = jnp.pad(env_row[:, :-1], ((0, 0), (1, 0), (0, 0), (0, 0)))
            mps_row = jnp.pad(mps_row[:-1], ((1, 0), (0, 0), (0, 0)))
        product = jnp.einsum("wdab,dbc->wdac", env_row, mps_row, preferred_element_type=jnp.float32)
        pieces.append(product.astype(jnp.bfloat16))
    return jnp.stack(pieces, axis=1)


def project_row(mixed_rows, charges, proj_padded, row_index):
    zero_index = jnp.zeros((), jnp.int32)

    def one_bond(inputs):
        mixed_bond, charge_bond = inputs
        term_list = []
        for phys_state in range(4):
            start_up = row_index + 2 - UP_CHARGE[phys_state] + charge_bond[0]
            start_down = 2 - DOWN_CHARGE[phys_state] + charge_bond[1]
            chosen = lax.dynamic_slice(
                proj_padded,
                (zero_index, start_up, start_down, zero_index, zero_index),
                (4, 1, DOWN_VALUES, BLOCK_DIM, BLOCK_DIM),
            )[:, 0]
            one_term = jnp.einsum(
                "tdij,dik->tdjk", chosen, mixed_bond[phys_state], preferred_element_type=jnp.float32
            )
            term_list.append(one_term.astype(jnp.bfloat16))
        return jnp.stack(term_list, axis=0)

    return lax.map(one_bond, (mixed_rows, charges))


def on_device(env_in, mps, proj, mpo, mpo_charge, block_sizes):
    chain_pos = lax.axis_index("chain")
    chain_count = lax.axis_size("chain")
    op_pos = lax.axis_index("op")
    local_bond = env_in.shape[0]
    left_sizes = lax.dynamic_index_in_dim(block_sizes, chain_pos, 0, keepdims=False)
    right_sizes = lax.dynamic_index_in_dim(block_sizes, chain_pos + 1, 0, keepdims=False)
    mps_grid, proj_grid = mask_site(mps[0], proj[0], left_sizes, right_sizes)
    proj_padded = jnp.pad(proj_grid, ((0, 0), (2, 2), (2, 2), (0, 0), (0, 0)))
    mpo_masked = mask_mpo(mpo[0], mpo_charge)
    local_charge = lax.dynamic_slice_in_dim(mpo_charge, op_pos * local_bond, local_bond, 0)
    local_mpo = lax.dynamic_slice_in_dim(mpo_masked, op_pos * local_bond, local_bond, 0)
    flat_local = jnp.transpose(local_mpo, (2, 0, 1, 3)).reshape(MPO_BOND, local_bond * 16)
    env_grid = env_in.reshape(local_bond, UP_VALUES, DOWN_VALUES, BLOCK_DIM, BLOCK_DIM)
    zero_row = jnp.zeros((local_bond, DOWN_VALUES, BLOCK_DIM, BLOCK_DIM), jnp.bfloat16)
    zero_all = jnp.zeros((local_bond, UP_VALUES, DOWN_VALUES, BLOCK_DIM, BLOCK_DIM), jnp.bfloat16)

    def compute_row(current, previous, row_index):
        mixed_rows = mix_row(current, previous, mps_grid, row_index)
        projected = project_row(mixed_rows, local_charge, proj_padded, row_index)
        flat_terms = projected.reshape(local_bond * 16, -1)
        summed = lax.psum_scatter(
            jnp.dot(flat_local, flat_terms, preferred_element_type=jnp.float32),
            "op",
            scatter_dimension=0,
            tiled=True,
        )
        return summed.astype(jnp.bfloat16).reshape(local_bond, DOWN_VALUES, BLOCK_DIM, BLOCK_DIM)

    def advance(step_index, loop_state):
        incoming, previous, collected = loop_state
        row_index = step_index - chain_pos
        active = (row_index >= 0) & (row_index < UP_VALUES)
        row_clipped = jnp.clip(row_index, 0, UP_VALUES - 1)
        first_row = lax.dynamic_index_in_dim(env_grid, row_clipped, 1, keepdims=False)
        first_row = jnp.where(active, first_row, zero_row)
        current = jnp.where(chain_pos == 0, first_row, incoming)
        new_row = compute_row(current, previous, row_clipped)
        new_row = jnp.where(active, new_row, zero_row)
        old_row = lax.dynamic_index_in_dim(collected, row_clipped, 1, keepdims=False)
        collected = lax.dynamic_update_index_in_dim(
            collected, jnp.where(active, new_row, old_row), row_clipped, 1
        )
        incoming = from_behind(new_row, "chain", 1)
        return (incoming, current, collected)

    final_state = lax.fori_loop(
        0, UP_VALUES + chain_count - 1, advance, (zero_row, zero_row, zero_all)
    )
    return final_state[2].reshape(1, local_bond, SECTORS, BLOCK_DIM, BLOCK_DIM)


def solution(mesh):
    return jax.shard_map(
        on_device,
        mesh=mesh,
        in_specs=(
            P("op", None, None, None),
            P("chain", None, None, None, None),
            P("chain", None, None, None, None),
            P("chain", None, None, None, None),
            P(),
            P(),
        ),
        out_specs=P("chain", "op", None, None, None),
        check_vma=False,
    )
```

profile of v0, /device:TPU:4, one launch (start us, length us, event | category | flops | bytes accessed | tf_op | source)
XLA Modules:
  0.0 1147.2 jit_solution(6347828204111570745)
XLA Ops:
  9.9 5.9 select_maximum_fusion
  18.3 1128.9 %while.63 = (s32[]{:T(128)}, bf16[2,2,128,128]{3,2,1,0:T(8,128)(2,1)S(1)}, bf16[2,2,128,128]{3,2,0,1:T(8,128)(2,1)S(1)}, bf16[2,8,2,128,128]{4,3,2,1,0:T(8,128)(...) while((s32[]{:T(128)}, ...), condition=%wide.region_4.5_spmd.clone, body=%wide.region_0.4_spmd.clone.sunk | while | flops 238927888 | bytes 25627140 | solution.py:160
  21.8 22.6 %while.64 = (s32[]{:T(128)}, bf16[2,4,4,2,128,128]{5,4,3,2,1,0:T(8,128)(2,1)}, bf16[2,4,2,128,128]{3,4,0,2,1:T(8,128)(2,1)S(1)}, s32[2,2]{1,0:T(2,128)S(1)}, s32...) while((s32[]{:T(128)}, ...), condition=%wide.region_2.2_spmd, body=%wide.region_1.1_spmd.sunk | while | flops 136314880 | bytes 9175941 | solution.py:111
  49.0 64.5 %all-reduce.10 = bf16[16,32768]{1,0:T(8,128)(2,1)S(1)} all-reduce(f32[16,32768]{1,0:T(8,128)} %convolution_bitcast_fusion.2), channel_id=2, replica_groups=mesh['chain'=4,'op'=8] {'op'}, use_global_device_ids=true, to_apply=%region_3.3.clone | all-reduce | flops 524288 | bytes 3145728 | tf_op jit(solution)/shard_map/while
  126.2 22.6 %while.64 = (s32[]{:T(128)}, bf16[2,4,4,2,128,128]{5,4,3,2,1,0:T(8,128)(2,1)}, bf16[2,4,2,128,128]{3,4,0,2,1:T(8,128)(2,1)S(1)}, s32[2,2]{1,0:T(2,128)S(1)}, s32...) while((s32[]{:T(128)}, ...), condition=%wide.region_2.2_spmd, body=%wide.region_1.1_spmd.sunk | while | flops 136314880 | bytes 9175941 | solution.py:111
  153.5 62.5 %all-reduce.10 = bf16[16,32768]{1,0:T(8,128)(2,1)S(1)} all-reduce(f32[16,32768]{1,0:T(8,128)} %convolution_bitcast_fusion.2), channel_id=2, replica_groups=mesh['chain'=4,'op'=8] {'op'}, use_global_device_ids=true, to_apply=%region_3.3.clone | all-reduce | flops 524288 | bytes 3145728 | tf_op jit(solution)/shard_map/while
  228.7 22.6 %while.64 = (s32[]{:T(128)}, bf16[2,4,4,2,128,128]{5,4,3,2,1,0:T(8,128)(2,1)}, bf16[2,4,2,128,128]{3,4,0,2,1:T(8,128)(2,1)S(1)}, s32[2,2]{1,0:T(2,128)S(1)}, s32...) while((s32[]{:T(128)}, ...), condition=%wide.region_2.2_spmd, body=%wide.region_1.1_spmd.sunk | while | flops 136314880 | bytes 9175941 | solution.py:111
  255.9 62.6 %all-reduce.10 = bf16[16,32768]{1,0:T(8,128)(2,1)S(1)} all-reduce(f32[16,32768]{1,0:T(8,128)} %convolution_bitcast_fusion.2), channel_id=2, replica_groups=mesh['chain'=4,'op'=8] {'op'}, use_global_device_ids=true, to_apply=%region_3.3.clone | all-reduce | flops 524288 | bytes 3145728 | tf_op jit(solution)/shard_map/while
  323.5 4.2 collective-permute-done
  331.1 22.6 %while.64 = (s32[]{:T(128)}, bf16[2,4,4,2,128,128]{5,4,3,2,1,0:T(8,128)(2,1)}, bf16[2,4,2,128,128]{3,4,0,2,1:T(8,128)(2,1)S(1)}, s32[2,2]{1,0:T(2,128)S(1)}, s32...) while((s32[]{:T(128)}, ...), condition=%wide.region_2.2_spmd, body=%wide.region_1.1_spmd.sunk | while | flops 136314880 | bytes 9175941 | solution.py:111
  358.4 62.5 %all-reduce.10 = bf16[16,32768]{1,0:T(8,128)(2,1)S(1)} all-reduce(f32[16,32768]{1,0:T(8,128)} %convolution_bitcast_fusion.2), channel_id=2, replica_groups=mesh['chain'=4,'op'=8] {'op'}, use_global_device_ids=true, to_apply=%region_3.3.clone | all-reduce | flops 524288 | bytes 3145728 | tf_op jit(solution)/shard_map/while
  425.9 4.2 collective-permute-done
  433.5 22.6 %while.64 = (s32[]{:T(128)}, bf16[2,4,4,2,128,128]{5,4,3,2,1,0:T(8,128)(2,1)}, bf16[2,4,2,128,128]{3,4,0,2,1:T(8,128)(2,1)S(1)}, s32[2,2]{1,0:T(2,128)S(1)}, s32...) while((s32[]{:T(128)}, ...), condition=%wide.region_2.2_spmd, body=%wide.region_1.1_spmd.sunk | while | flops 136314880 | bytes 9175941 | solution.py:111
  460.8 62.6 %all-reduce.10 = bf16[16,32768]{1,0:T(8,128)(2,1)S(1)} all-reduce(f32[16,32768]{1,0:T(8,128)} %convolution_bitcast_fusion.2), channel_id=2, replica_groups=mesh['chain'=4,'op'=8] {'op'}, use_global_device_ids=true, to_apply=%region_3.3.clone | all-reduce | flops 524288 | bytes 3145728 | tf_op jit(solution)/shard_map/while
  528.4 4.2 collective-permute-done
  536.0 22.6 %while.64 = (s32[]{:T(128)}, bf16[2,4,4,2,128,128]{5,4,3,2,1,0:T(8,128)(2,1)}, bf16[2,4,2,128,128]{3,4,0,2,1:T(8,128)(2,1)S(1)}, s32[2,2]{1,0:T(2,128)S(1)}, s32...) while((s32[]{:T(128)}, ...), condition=%wide.region_2.2_spmd, body=%wide.region_1.1_spmd.sunk | while | flops 136314880 | bytes 9175941 | solution.py:111
  563.2 62.5 %all-reduce.10 = bf16[16,32768]{1,0:T(8,128)(2,1)S(1)} all-reduce(f32[16,32768]{1,0:T(8,128)} %convolution_bitcast_fusion.2), channel_id=2, replica_groups=mesh['chain'=4,'op'=8] {'op'}, use_global_device_ids=true, to_apply=%region_3.3.clone | all-reduce | flops 524288 | bytes 3145728 | tf_op jit(solution)/shard_map/while
  630.8 4.2 collective-permute-done
  638.4 22.6 %while.64 = (s32[]{:T(128)}, bf16[2,4,4,2,128,128]{5,4,3,2,1,0:T(8,128)(2,1)}, bf16[2,4,2,128,128]{3,4,0,2,1:T(8,128)(2,1)S(1)}, s32[2,2]{1,0:T(2,128)S(1)}, s32...) while((s32[]{:T(128)}, ...), condition=%wide.region_2.2_spmd, body=%wide.region_1.1_spmd.sunk | while | flops 136314880 | bytes 9175941 | solution.py:111
  665.6 62.6 %all-reduce.10 = bf16[16,32768]{1,0:T(8,128)(2,1)S(1)} all-reduce(f32[16,32768]{1,0:T(8,128)} %convolution_bitcast_fusion.2), channel_id=2, replica_groups=mesh['chain'=4,'op'=8] {'op'}, use_global_device_ids=true, to_apply=%region_3.3.clone | all-reduce | flops 524288 | bytes 3145728 | tf_op jit(solution)/shard_map/while
  733.3 4.2 collective-permute-done
  740.9 22.6 %while.64 = (s32[]{:T(128)}, bf16[2,4,4,2,128,128]{5,4,3,2,1,0:T(8,128)(2,1)}, bf16[2,4,2,128,128]{3,4,0,2,1:T(8,128)(2,1)S(1)}, s32[2,2]{1,0:T(2,128)S(1)}, s32...) while((s32[]{:T(128)}, ...), condition=%wide.region_2.2_spmd, body=%wide.region_1.1_spmd.sunk | while | flops 136314880 | bytes 9175941 | solution.py:111
  768.1 62.5 %all-reduce.10 = bf16[16,32768]{1,0:T(8,128)(2,1)S(1)} all-reduce(f32[16,32768]{1,0:T(8,128)} %convolution_bitcast_fusion.2), channel_id=2, replica_groups=mesh['chain'=4,'op'=8] {'op'}, use_global_device_ids=true, to_apply=%region_3.3.clone | all-reduce | flops 524288 | bytes 3145728 | tf_op jit(solution)/shard_map/while
  835.7 4.2 collective-permute-done
  843.3 22.6 %while.64 = (s32[]{:T(128)}, bf16[2,4,4,2,128,128]{5,4,3,2,1,0:T(8,128)(2,1)}, bf16[2,4,2,128,128]{3,4,0,2,1:T(8,128)(2,1)S(1)}, s32[2,2]{1,0:T(2,128)S(1)}, s32...) while((s32[]{:T(128)}, ...), condition=%wide.region_2.2_spmd, body=%wide.region_1.1_spmd.sunk | while | flops 136314880 | bytes 9175941 | solution.py:111
  870.5 62.6 %all-reduce.10 = bf16[16,32768]{1,0:T(8,128)(2,1)S(1)} all-reduce(f32[16,32768]{1,0:T(8,128)} %convolution_bitcast_fusion.2), channel_id=2, replica_groups=mesh['chain'=4,'op'=8] {'op'}, use_global_device_ids=true, to_apply=%region_3.3.clone | all-reduce | flops 524288 | bytes 3145728 | tf_op jit(solution)/shard_map/while
  938.2 4.2 collective-permute-done
  945.8 22.6 %while.64 = (s32[]{:T(128)}, bf16[2,4,4,2,128,128]{5,4,3,2,1,0:T(8,128)(2,1)}, bf16[2,4,2,128,128]{3,4,0,2,1:T(8,128)(2,1)S(1)}, s32[2,2]{1,0:T(2,128)S(1)}, s32...) while((s32[]{:T(128)}, ...), condition=%wide.region_2.2_spmd, body=%wide.region_1.1_spmd.sunk | while | flops 136314880 | bytes 9175941 | solution.py:111
  973.0 62.5 %all-reduce.10 = bf16[16,32768]{1,0:T(8,128)(2,1)S(1)} all-reduce(f32[16,32768]{1,0:T(8,128)} %convolution_bitcast_fusion.2), channel_id=2, replica_groups=mesh['chain'=4,'op'=8] {'op'}, use_global_device_ids=true, to_apply=%region_3.3.clone | all-reduce | flops 524288 | bytes 3145728 | tf_op jit(solution)/shard_map/while
  1040.6 4.2 collective-permute-done
  1048.2 22.6 %while.64 = (s32[]{:T(128)}, bf16[2,4,4,2,128,128]{5,4,3,2,1,0:T(8,128)(2,1)}, bf16[2,4,2,128,128]{3,4,0,2,1:T(8,128)(2,1)S(1)}, s32[2,2]{1,0:T(2,128)S(1)}, s32...) while((s32[]{:T(128)}, ...), condition=%wide.region_2.2_spmd, body=%wide.region_1.1_spmd.sunk | while | flops 136314880 | bytes 9175941 | solution.py:111
  1075.4 62.6 %all-reduce.10 = bf16[16,32768]{1,0:T(8,128)(2,1)S(1)} all-reduce(f32[16,32768]{1,0:T(8,128)} %convolution_bitcast_fusion.2), channel_id=2, replica_groups=mesh['chain'=4,'op'=8] {'op'}, use_global_device_ids=true, to_apply=%region_3.3.clone | all-reduce | flops 524288 | bytes 3145728 | tf_op jit(solution)/shard_map/while
  (465 shorter events, 319.5 us)
Async XLA Ops:
  0.0 6.7 copy-start.2
  0.0 6.7 copy-start.3
  0.0 6.6 copy-start.1
  7.7 8.3 copy-start
  9.6 8.7 copy-start.4
  115.0 7.8 collective-permute-start
  217.5 7.8 collective-permute-start
  319.9 7.8 collective-permute-start
  422.4 7.8 collective-permute-start
  524.8 7.8 collective-permute-start
  627.2 7.8 collective-permute-start
  729.7 7.8 collective-permute-start
  832.1 7.8 collective-permute-start
  934.6 7.8 collective-permute-start
  1037.0 7.8 collective-permute-start
  1139.5 7.8 collective-permute-start
where the time goes:
time: 1150 us
  blocking collectives  690 us (60%)
  matrix products  139 us (12%)
  local copies, waits for them, and re-layouts  110 us (10%)
  loops' own time  98.2 us (9%)
  waiting for transfers between devices  44.2 us (4%)
  other arithmetic  42.5 us (4%)
  starting transfers between devices  23.2 us (2%)
    while x11, blocking collectives  690 us
    dot_general x88, matrix products, one_bond(): jnp.einsum('tdij,dik->tdjk', chosen, mixed_bond[phys_state], preferred_el...  103 us
    another operation x11, loops' own time, project_row(): return lax.map(one_bond, (mixed_rows, charges))  90.1 us
    ppermute x11, waiting for transfers between devices, from_behind(): return lax.ppermute(block, axis, route)  44.2 us
    dynamic_update_slice x44, local copies, waits for them, and re-layouts, project_row(): return lax.map(one_bond, (mixed_rows, charges))  37.7 us
    reshape x11, local copies, waits for them, and re-layouts, compute_row(): flat_terms = projected.reshape(local_bond * 16, -1)  31 us
    ppermute x11, starting transfers between devices, from_behind(): return lax.ppermute(block, axis, route)  23.2 us
  transfers between devices with their start and end apart: 11, of which 11 were waited for; matrix products, arithmetic and copies ran while one was open for 2% of the time, Pallas kernels for 0%

commit v1 on v0

v1 whole, which is shorter than its diff:
```python
import functools

import jax
import jax.numpy as jnp
from jax import lax
from jax.experimental import pallas as pl
from jax.experimental.pallas import tpu as pltpu
from jax.sharding import PartitionSpec as P


UP_VALUES = 8
DOWN_VALUES = 2
PHYS = 4

UP_CHARGE = (0, 1, 0, 1)
DOWN_CHARGE = (0, 0, 1, 1)

STATE_ORDER = (0, 2, 1, 3)
MPS_PARTS = ((0, 0, 2), (2, 0, 1), (1, -1, 2), (3, -1, 1))
MPS_BLOCKS = ((0, 0, 0), (0, 0, 1), (2, 0, 0), (1, -1, 0), (1, -1, 1), (3, -1, 0))
ROW_SHIFTS = 3
PROJ_PARTS = ((0, -1, 2), (1, -2, 2), (2, -1, 1), (3, -2, 1))
GROUP = 8


VMEM = pl.BlockSpec(memory_space=pltpu.VMEM)
SMEM = pl.BlockSpec(memory_space=pltpu.SMEM)
ANY = pl.BlockSpec(memory_space=pl.ANY)
HBM = pl.BlockSpec(memory_space=pltpu.HBM)


def ring_chain(position, count):
    turned = (position + count - 1) % count
    return turned ^ (turned >> 1)


def place(chain, count):
    plain = chain ^ (chain >> 1) ^ (chain >> 2)
    return (plain + 1) % count if isinstance(chain, int) else lax.rem(plain + 1, count)


def my_row(chain_count, spread):
    side = lax.rem(lax.axis_index("op"), spread)
    return place(lax.axis_index("chain"), chain_count) * spread + side


def held_rows(spread):
    return -(-(ROW_SHIFTS + spread - 1) // spread)


def held_base(first_row, offset, holder, spread):
    rows = held_rows(spread)
    return jnp.clip(first_row + offset + holder * rows, 0, UP_VALUES - rows)


def proj_start(phys_state, spread):
    start = len(MPS_BLOCKS)
    for part_state, _, downs in PROJ_PARTS:
        if part_state == phys_state:
            return start
        start += held_rows(spread) * downs
    return start


def mpo_matrix(site_mpo):
    bond = site_mpo.shape[0]
    ordered = jnp.stack([site_mpo[:, state] for state in STATE_ORDER], axis=1)
    return jnp.transpose(ordered, (2, 3, 1, 0)).reshape(bond * PHYS, PHYS * bond)


def call(kernel, *args, **options):
    return plain_call(kernel, *args, **options)


def plain_call(kernel, out_shape, specs, operands, scratch=(), limit=20, flops=10**8):
    one = not isinstance(out_shape, (list, tuple))
    return pl.pallas_call(
        kernel,
        out_shape=out_shape,
        in_specs=specs,
        out_specs=VMEM if one else tuple(VMEM for _ in out_shape),
        scratch_shapes=list(scratch),
        compiler_params=pltpu.CompilerParams(vmem_limit_bytes=limit << 20),
        cost_estimate=pl.CostEstimate(flops=flops, bytes_accessed=10**6, transcendentals=0),
    )(*operands)


def shape_of(*dims, dtype=jnp.bfloat16):
    return jax.ShapeDtypeStruct(dims, dtype)


def run_copies(copies):
    for copy in copies:
        copy.start()
    for copy in copies:
        copy.wait()


def pack_env_kernel(chain_count, spread, env_ref, out_ref, sem):
    first = place(lax.axis_index("chain"), chain_count) * spread
    before = jnp.maximum(first - 1, 0)
    copies = []

    def add(source, target):
        copies.append(pltpu.make_async_copy(source, target, sem.at[len(copies)]))

    for bond in range(env_ref.shape[0]):
        add(env_ref.at[bond, pl.ds(before, 1)], out_ref.at[bond, pl.ds(0, 1)])
        add(env_ref.at[bond, pl.ds(first, spread)], out_ref.at[bond, pl.ds(1, spread)])
    run_copies(copies)


def pack_site_kernel(chain_count, spread, mps_ref, proj_ref, matrix_ref, *refs):
    out_refs, sem = refs[:-1], refs[-1]
    chain_pos = lax.axis_index("chain")
    side = lax.rem(lax.axis_index("op"), spread)
    copies = []

    def add(source, target):
        copies.append(pltpu.make_async_copy(source, target, sem.at[len(copies)]))

    rows = held_rows(spread)
    for hop, out_ref in enumerate(out_refs):
        first = place(jnp.bitwise_xor(chain_pos, hop), chain_count) * spread
        start = 0
        for phys_state, offset, downs in MPS_PARTS:
            sector = jnp.maximum(first + side + offset, 0) * DOWN_VALUES
            add(
                mps_ref.at[0, phys_state, pl.ds(sector, downs)],
                out_ref.at[pl.ds(start, downs)],
            )
            start += downs
        for phys_state, offset, downs in PROJ_PARTS:
            base = held_base(first, offset, side, spread)
            start = proj_start(phys_state, spread)
            for down in range(downs):
                add(
                    proj_ref.at[0, phys_state, pl.ds(base, rows), down],
                    out_ref.at[pl.ds(start + down * rows, rows)],
                )
        out_ref[out_ref.shape[0] - 1, : matrix_ref.shape[0]] = matrix_ref[...]
    run_copies(copies)


def mask_kernel(charges, out_ref):
    rows, lanes = out_ref.shape
    bond = rows // PHYS
    row_at = lax.broadcasted_iota(jnp.int32, (rows, lanes), 0)
    lane_at = lax.broadcasted_iota(jnp.int32, (rows, lanes), 1)
    ones = jnp.ones((rows, lanes), jnp.float32)
    for axis, table in enumerate((UP_CHARGE, DOWN_CHARGE)):
        left = jnp.zeros((rows, lanes), jnp.int32)
        right = jnp.zeros((rows, lanes), jnp.int32)
        for index in range(bond):
            value = charges[index, axis]
            left = jnp.where(row_at // PHYS == index, value, left)
            right = jnp.where(lane_at % bond == index, value, right)
        for index in range(PHYS):
            left = left - jnp.where(row_at % PHYS == index, table[index], 0)
            right = right - jnp.where(lane_at // bond == index, table[STATE_ORDER[index]], 0)
        ones = jnp.where(left == right, ones, 0.0)
    out_ref[...] = ones


def prep_kernel(site, chain_count, spread, bond, block, slots, sizes, mask, *refs):
    weight_refs = refs[: slots * spread]
    mps_ref, turned, kron, weights, sem = refs[slots * spread :]
    row = my_row(chain_count, spread)
    side = lax.rem(lax.axis_index("op"), spread)
    slot = jnp.bitwise_xor(lax.axis_index("chain"), site)
    for index in range(slots):
        @pl.when(slot == index)
        def _():
            run_copies(
                [
                    pltpu.make_async_copy(
                        weight_refs[index * spread + turn],
                        weights.at[jnp.bitwise_xor(side, turn)],
                        sem.at[turn],
                    )
                    for turn in range(spread)
                ]
            )

    row_at = lax.broadcasted_iota(jnp.int32, (block, block), 0)
    column_at = lax.broadcasted_iota(jnp.int32, (block, block), 1)
    for index, (phys_state, offset, down) in enumerate(MPS_BLOCKS):
        source = jnp.maximum(row + offset, 0) * DOWN_VALUES + down
        target = row * DOWN_VALUES + down + DOWN_CHARGE[phys_state]
        high = jnp.where(row + offset >= 0, sizes[site, source], 0)
        keep = (row_at < high) & (column_at < sizes[site + 1, target])
        value = weights[side, index]
        mps_ref[index] = jnp.where(keep, value, jnp.zeros_like(value))

    held = held_rows(spread)
    turned[...] = jnp.zeros_like(turned)
    for phys_state, offset, _ in PROJ_PARTS:
        for shift in range(ROW_SHIFTS):
            for target in range(DOWN_VALUES):
                down = target - DOWN_CHARGE[phys_state]
                if down < 0:
                    continue
                wanted = row + offset + shift
                holder = (side + shift) // held
                base = held_base(row - side, offset, holder, spread)
                at = jnp.clip(wanted - base, 0, held - 1)
                at = proj_start(phys_state, spread) + down * held + at
                value = weights[holder, at].T
                inside = (wanted >= 0) & (wanted < UP_VALUES)
                turned[
                    shift * DOWN_VALUES + target,
                    :,
                    phys_state * block : (phys_state + 1) * block,
                ] = jnp.where(inside, value, jnp.zeros_like(value))

    pairs = bond * PHYS
    wide = pairs * GROUP
    matrix = weights[side, weights.shape[1] - 1, :pairs, :].astype(jnp.float32)
    matrix = jnp.where(mask[...] > 0.5, matrix, 0.0).astype(jnp.bfloat16)
    lanes = matrix.shape[1]
    tall = (
        lax.broadcasted_iota(jnp.int32, (wide, pairs), 0) // GROUP
        == lax.broadcasted_iota(jnp.int32, (wide, pairs), 1)
    ).astype(jnp.bfloat16)
    across = (
        lax.broadcasted_iota(jnp.int32, (lanes, wide), 0)
        == lax.broadcasted_iota(jnp.int32, (lanes, wide), 1) // GROUP
    ).astype(jnp.bfloat16)
    spread_out = jnp.dot(tall, matrix, preferred_element_type=jnp.float32).astype(jnp.bfloat16)
    spread_out = jnp.dot(spread_out, across, preferred_element_type=jnp.float32)
    same = (
        lax.broadcasted_iota(jnp.int32, (wide, wide), 0) % GROUP
        == lax.broadcasted_iota(jnp.int32, (wide, wide), 1) % GROUP
    )
    kron[...] = jnp.where(same, spread_out, 0.0).astype(jnp.bfloat16)


def mix(mixed, pieces, right, at):
    block = right.shape[0]
    for first, rows in pieces:
        count = rows.shape[0]
        product = jnp.dot(
            rows.reshape(count * block, block), right, preferred_element_type=jnp.float32
        )
        mixed[pl.ds(at + first, count)] = product.reshape(count, block, block)


def contract(mixed, used, kron, row_at, rows, column_at, store):
    block = mixed.shape[-1]

    def body(index, carry):
        at = pl.multiple_of(index * 2 * GROUP, 2 * GROUP)
        low = mixed[:used, pl.ds(at, GROUP), :].reshape(used * GROUP, block)
        high = mixed[:used, pl.ds(at + GROUP, GROUP), :].reshape(used * GROUP, block)
        right = jnp.concatenate([low, high], axis=1).astype(jnp.bfloat16)
        left = kron[pl.ds(row_at, rows), column_at : column_at + used * GROUP]
        got = jnp.dot(left, right, preferred_element_type=jnp.float32)
        store(
            at,
            got[:, :block].reshape(rows // GROUP, GROUP, block),
            got[:, block:].reshape(rows // GROUP, GROUP, block),
        )
        return carry

    steps = block // (2 * GROUP)
    lax.fori_loop(0, steps, body, 0, unroll=steps)


def pieces_of(env_refs, offset, down, spread, per_chunk):
    if len(env_refs) == 1:
        return [(0, env_refs[0][:, down])]
    op_pos = lax.axis_index("op")
    side = lax.rem(op_pos, spread)
    return [
        (jnp.bitwise_xor(op_pos, index) * per_chunk, ref[:, side + 1 + offset, down])
        for index, ref in enumerate(env_refs)
    ]


def left_rows(pairs, kept_rows, spread):
    if kept_rows == pairs:
        return 0
    layer = lax.axis_index("op") // spread
    return pl.multiple_of(layer * (kept_rows * GROUP), kept_rows * GROUP)


def own_kernel(spread, bond, kept_rows, chunks, mps_ref, kron, *refs):
    env_refs, (out_ref, mixed) = refs[:chunks], refs[chunks:]
    pairs = bond * PHYS
    per_chunk = bond // chunks
    at_row = left_rows(pairs, kept_rows, spread)
    for down in range(DOWN_VALUES):
        mix(mixed, pieces_of(env_refs, 0, down, spread, per_chunk), mps_ref[down], 0)
        used = bond
        if down:
            mix(mixed, pieces_of(env_refs, 0, 0, spread, per_chunk), mps_ref[2], bond)
            used = 2 * bond

        def store(at, low, high):
            out_ref[down, :, pl.ds(at, GROUP), :] = low
            out_ref[down, :, pl.ds(at + GROUP, GROUP), :] = high

        contract(mixed, used, kron, at_row, kept_rows * GROUP, 0, store)


def main_kernel(
    chain_count, spread, bond, kept_rows, chunks, others, charges, mps_ref, turned, kron,
    own_ref, *refs
):
    env_refs, refs = refs[:chunks], refs[chunks:]
    kept_refs, refs = refs[:others], refs[others:]
    mixed, summed, result = refs[-3:]
    out_refs = refs[:-3]
    block = mps_ref.shape[-1]
    pairs = bond * PHYS
    per_chunk = bond // chunks
    row = my_row(chain_count, spread)
    at_row = left_rows(pairs, kept_rows, spread)
    last = kept_rows != pairs
    kept_bonds = kept_rows // PHYS
    layer = lax.axis_index("op") // spread
    for down in range(DOWN_VALUES):
        mix(mixed, pieces_of(env_refs, -1, down, spread, per_chunk), mps_ref[3 + down], 0)
        used = bond
        if down:
            mix(mixed, pieces_of(env_refs, -1, 0, spread, per_chunk), mps_ref[5], bond)
            used = 2 * bond

        def store(at, low, high):
            summed[:, pl.ds(at, GROUP), :] = low + own_ref[down, :, pl.ds(at, GROUP), :]
            summed[:, pl.ds(at + GROUP, GROUP), :] = (
                high + own_ref[down, :, pl.ds(at + GROUP, GROUP), :]
            )

        contract(mixed, used, kron, at_row, kept_rows * GROUP, 2 * bond * GROUP, store)
        for index in range(kept_bonds):
            bond_index = layer * kept_bonds + index if last else index
            up = charges[bond_index, 0]
            target = down + charges[bond_index, 1]
            inside = (
                (row + up >= 0)
                & (row + up < UP_VALUES)
                & (target >= 0)
                & (target < DOWN_VALUES)
            )
            entry = jnp.where(
                inside, (up + 1) * DOWN_VALUES + target, ROW_SHIFTS * DOWN_VALUES
            )
            right = (
                summed[index * PHYS : (index + 1) * PHYS]
                .reshape(PHYS * block, block)
                .astype(jnp.bfloat16)
            )
            value = jnp.dot(turned[entry], right, preferred_element_type=jnp.float32)
            value = value.astype(jnp.bfloat16)
            if last:
                result[index, down] = value
            else:
                out_refs[0][index, down] = value
    if not last:
        count = out_refs[1].shape[0]
        out_refs[1][...] = out_refs[0][pl.ds(layer * count, count)]
        return
    chain_pos = lax.axis_index("chain")
    side = lax.rem(lax.axis_index("op"), spread)
    count = kept_bonds // spread
    sources = list(kept_refs) + [result]
    for hop in range(chain_count):
        target_chain = jnp.bitwise_xor(chain_pos, hop)
        for turn in range(spread):
            first = jnp.bitwise_xor(side, turn) * count
            for source_site, source in enumerate(sources):
                @pl.when(target_chain == source_site)
                def _():
                    out_refs[hop * spread + turn][...] = source[pl.ds(first, count)]


def gather_kernel(chain_count, spread, *refs):
    out_ref = refs[-1]
    chain_pos = lax.axis_index("chain")
    side = lax.rem(lax.axis_index("op"), spread)
    for hop in range(chain_count):
        for turn in range(spread):
            row = place(jnp.bitwise_xor(chain_pos, hop), chain_count) * spread
            row = row + jnp.bitwise_xor(side, turn)
            out_ref[0, :, pl.ds(row * DOWN_VALUES, DOWN_VALUES)] = refs[hop * spread + turn][...]


def sweep(env_in, mps, proj, mpo, mpo_charge, block_sizes):
    chain_count = lax.axis_size("chain")
    op_count = lax.axis_size("op")
    local_bond, sectors, block, _ = env_in.shape
    bond = mpo_charge.shape[0]
    pairs = bond * PHYS
    sites = block_sizes.shape[0] - 1
    spread = UP_VALUES // chain_count
    both = ("chain", "op")
    everyone = [(c, o) for c in range(chain_count) for o in range(op_count)]
    square = (block, block)

    def flat(chain, op):
        return chain * op_count + op

    packed = call(
        functools.partial(pack_env_kernel, chain_count, spread),
        shape_of(local_bond, spread + 1, DOWN_VALUES, *square),
        [HBM],
        [env_in.reshape(local_bond, UP_VALUES, DOWN_VALUES, *square)],
        [pltpu.SemaphoreType.DMA((2 * local_bond,))],
        limit=60,
    )
    received = [packed]
    for hop in range(spread, op_count, spread):
        received.append(lax.ppermute(packed, "op", [(o, o ^ hop) for o in range(op_count)]))
    chunks = []
    for piece in received:
        chunks.append(piece)
        for turn in range(1, spread):
            chunks.append(lax.ppermute(piece, "op", [(o, o ^ turn) for o in range(op_count)]))

    matrix = mpo_matrix(mpo[0])
    matrix = jnp.pad(matrix, ((0, 0), (0, block - matrix.shape[1])))
    blocks = proj_start(None, spread) + 1
    far = chain_count - 1
    moves = chain_count * (len(MPS_PARTS) + sum(part[2] for part in PROJ_PARTS))
    parcels = call(
        functools.partial(pack_site_kernel, chain_count, spread),
        [shape_of(blocks, *square)] * chain_count,
        [HBM, HBM, VMEM],
        [
            mps,
            proj.reshape(1, PHYS, UP_VALUES, DOWN_VALUES, *square),
            matrix,
        ],
        [pltpu.SemaphoreType.DMA((moves,))],
        limit=60,
    )
    weights = [parcels[0]]
    for hop in range(1, far):
        weights.append(
            lax.ppermute(parcels[hop], "chain", [(c, c ^ hop) for c in range(chain_count)])
        )
    weights.append(lax.ppermute(parcels[far], "chain", [(0, far)]))
    weights.append(
        lax.ppermute(parcels[far], "chain", [(c, c ^ far) for c in range(1, chain_count)])
    )
    turned_weights = []
    for piece in weights:
        turned_weights.append(
            [piece]
            + [
                lax.ppermute(piece, "op", [(o, o ^ turn) for o in range(op_count)])
                for turn in range(1, spread)
            ]
        )
    weights = turned_weights
    mask = call(mask_kernel, shape_of(pairs, block, dtype=jnp.float32), [SMEM], [mpo_charge])

    halo = []
    for c, o in everyone:
        at = place(c, chain_count)
        if o % spread < spread - 1:
            halo.append((flat(c, o), flat(c, o + 1)))
        elif at < chain_count - 1:
            halo.append((flat(c, o), flat(ring_chain(at + 1, chain_count), o - spread + 1)))

    keep = local_bond * spread
    kept = []
    own_env = prev_env = chunks
    for site in range(sites):
        last = site == sites - 1
        kept_rows = keep * PHYS if last else pairs
        count = len(own_env)
        masked, turned, kron = call(
            functools.partial(
                prep_kernel, site, chain_count, spread, bond, block, chain_count
            ),
            [
                shape_of(len(MPS_BLOCKS), *square),
                shape_of(ROW_SHIFTS * DOWN_VALUES + 1, block, PHYS * block),
                shape_of(pairs * GROUP, pairs * GROUP),
            ],
            [SMEM, VMEM] + [ANY] * (chain_count * spread),
            [block_sizes, mask]
            + sum(weights[:far], [])
            + weights[far + 1 if site else far],
            [
                pltpu.VMEM((spread, blocks, *square), jnp.bfloat16),
                pltpu.SemaphoreType.DMA((spread,)),
            ],
        )
        own = call(
            functools.partial(own_kernel, spread, bond, kept_rows, count),
            shape_of(DOWN_VALUES, kept_rows, *square, dtype=jnp.float32),
            [VMEM] * (2 + count),
            [masked, kron] + own_env,
            [pltpu.VMEM((2 * bond, *square), jnp.float32)],
        )
        if last:
            out = [shape_of(local_bond, DOWN_VALUES, *square)] * (chain_count * spread)
        else:
            out = [shape_of(bond, DOWN_VALUES, *square), shape_of(keep, DOWN_VALUES, *square)]
        others = kept if last else []
        results = call(
            functools.partial(
                main_kernel, chain_count, spread, bond, kept_rows, count, len(others)
            ),
            out,
            [SMEM] + [VMEM] * (4 + count + len(others)),
            [mpo_charge, masked, turned, kron, own] + prev_env + others,
            [
                pltpu.VMEM((2 * bond, *square), jnp.float32),
                pltpu.VMEM((kept_rows, *square), jnp.float32),
                pltpu.VMEM((keep, DOWN_VALUES, *square), jnp.bfloat16),
            ],
            limit=28,
        )
        if not last:
            kept.append(results[1])
            own_env = [results[0]]
            prev_env = [lax.ppermute(results[0], both, halo)]

    arrived = []
    for hop in range(chain_count):
        for turn in range(spread):
            piece = results[hop * spread + turn]
            if hop or turn:
                piece = lax.ppermute(
                    piece, both, [(flat(c, o), flat(c ^ hop, o ^ turn)) for c, o in everyone]
                )
            arrived.append(piece)
    return call(
        functools.partial(gather_kernel, chain_count, spread),
        shape_of(1, local_bond, sectors, *square),
        [VMEM] * len(arrived),
        arrived,
    )


def solution(mesh):
    return jax.shard_map(
        sweep,
        mesh=mesh,
        in_specs=(
            P("op", None, None, None),
            P("chain", None, None, None, None),
            P("chain", None, None, None, None),
            P("chain", None, None, None, None),
            P(),
            P(),
        ),
        out_specs=P("chain", "op", None, None, None),
        check_vma=False,
    )
```

time: 1150 us -> 154 us (0.13)
  the two profiles are of different devices: /device:TPU:4 before, /device:TPU:15 now
where the time goes in v1:
time: 154 us; the launch traced here: 153 us
  waiting for transfers between devices  63.3 us (41%)
  starting transfers between devices  41.9 us (27%)
  Pallas kernels  40.1 us (26%)
  local copies, waits for them, and re-layouts  7.08 us (5%)
    pallas_call x16, Pallas kernels, plain_call(): pl.pallas_call(kernel, out_shape=out_shape, in_specs=specs, out_specs=VME...  40.1 us
    ppermute x3, waiting for transfers between devices, sweep(): lax.ppermute(packed, 'op', [(o, o ^ hop) for o in range(op_count)])  31.3 us
    ppermute x3, waiting for transfers between devices, sweep(): prev_env = [lax.ppermute(results[0], both, halo)]  18.3 us
    ppermute x7, starting transfers between devices, sweep(): lax.ppermute(piece, both, [(flat(c, o), flat(c ^ hop, o ^ turn)) for c, o...  16.7 us
    ppermute x9, starting transfers between devices, sweep(): lax.ppermute(piece, 'op', [(o, o ^ turn) for o in range(op_count)])  13.5 us
    ppermute x7, waiting for transfers between devices, sweep(): lax.ppermute(piece, both, [(flat(c, o), flat(c ^ hop, o ^ turn)) for c, o...  10.7 us
    unnamed x17, local copies, waits for them, and re-layouts  5.43 us
    ppermute x3, starting transfers between devices, sweep(): lax.ppermute(packed, 'op', [(o, o ^ hop) for o in range(op_count)])  3.9 us
  transfers between devices with their start and end apart: 26, of which 8 were waited for; matrix products, arithmetic and copies ran while one was open for 0% of the time, Pallas kernels for 16%

profile of v1, /device:TPU:15, one launch (start us, length us, event | category | flops | bytes accessed | tf_op | source)
XLA Modules:
  0.0 152.8 jit_solution(4996690326057486631)
XLA Ops:
  1.7 4.2 %shard_map.65 = (bf16[19,128,128]{2,1,0:T(8,128)(2,1)}, bf16[19,128,128]{2,1,0:T(8,128)(2,1)}, bf16[19,128,128]{2,1,0:T(8,128)(2,1)}, bf16[19,128,128]{2,1,0:T(8,128)(2,1)}) custom-call(bf16[1,4,16,128,128]{4,3,2,1,0:T(8,128)(2,1)} %mps_ref.1, bf16[1,4,8,2,128,128]{5,4,3,2,1,0:T(8,128)(2,1)} %bitcast.5, bf16[64,128]{1,0:T(8,128)(2,1)} %pad.4.matrix_ref), custom_call_target="tpu_custom_call" | custom-call | flops 100000000 | bytes 1000000 | tf_op jit(solution)/shard_map/pallas_call | solution.py:77
  7.8 1.8 %shard_map.70.refs_0_ = bf16[2,3,2,128,128]{4,3,2,1,0:T(8,128)(2,1)} custom-call(bf16[2,8,2,128,128]{4,3,2,1,0:T(8,128)(2,1)} %bitcast.6), custom_call_target="tpu_custom_call" | custom-call | flops 100000000 | bytes 1000000 | tf_op jit(solution)/shard_map/pallas_call | solution.py:77
  9.7 2.5 %collective-permute-start.12 = (bf16[2,3,2,128,128]{4,3,2,1,0:T(8,128)(2,1)}, bf16[2,3,2,128,128]{4,3,2,1,0:T(8,128)(2,1)}, u32[]{:S(2)}, u32[]{:S(2)}) collective-permute-start(bf16[2,3,2,128,128]{4,3,2,1,0:T(8,128)(2,1)} %shard_map.70.refs_0_), channel_id=1, source_target_pairs={{0,4},{1,5},{2,6},{3,7},{4,0},{5,1},{6,2},{7,3},{8,12},{9,13},{10,... | collective-permute-start | bytes 1179656 | tf_op jit(solution)/shard_map/ppermute | solution.py:414
  12.2 13.7 %collective-permute-done.10.refs_2_ = bf16[2,3,2,128,128]{4,3,2,1,0:T(8,128)(2,1)S(1)} collective-permute-done((bf16[2,3,2,128,128]{4,3,2,1,0:T(8,128)(2,1)}, bf16[2,3,2,128,128]{4,3,2,1,0:T(8,128)(2,1)S(1)}, u32[]{:S(2)}, u32[]{:S(2)}) %collective-permute-start.10) | collective-permute-done | bytes 393248 | tf_op jit(solution)/shard_map/ppermute | solution.py:414
  25.8 1.8 %collective-permute-start = (bf16[19,128,128]{2,1,0:T(8,128)(2,1)}, bf16[19,128,128]{2,1,0:T(8,128)(2,1)S(1)}, u32[]{:S(2)}, u32[]{:S(2)}) collective-permute-start(bf16[19,128,128]{2,1,0:T(8,128)(2,1)} %get-tuple-element.35.refs_0_), channel_id=1, source_target_pairs={{0,1},{1,0},{2,3},{3,2},{4,5},{5,4},{6,7},{7,6},{8,9},{9,8},{10,11... | collective-permute-start | bytes 1867784 | tf_op jit(solution)/shard_map/ppermute | solution.py:452
  27.6 8.6 %collective-permute-start.4 = (bf16[19,128,128]{2,1,0:T(8,128)(2,1)S(1)}, bf16[19,128,128]{2,1,0:T(8,128)(2,1)S(1)}, u32[]{:S(2)}, u32[]{:S(2)}) collective-permute-start(bf16[19,128,128]{2,1,0:T(8,128)(2,1)S(1)} %collective-permute-done.3.refs_4_), channel_id=1, source_target_pairs={{0,1},{1,0},{2,3},{3,2},{4,5},{5,4},{6,7},{7,6},{8,9},{9,8},{10,11... | collective-permute-start | bytes 1867784 | tf_op jit(solution)/shard_map/ppermute | solution.py:452
  36.3 1.4 collective-permute-start.14
  37.6 17.7 %collective-permute-done.14.refs_6_ = bf16[2,3,2,128,128]{4,3,2,1,0:T(8,128)(2,1)} collective-permute-done((bf16[2,3,2,128,128]{4,3,2,1,0:T(8,128)(2,1)}, bf16[2,3,2,128,128]{4,3,2,1,0:T(8,128)(2,1)}, u32[]{:S(2)}, u32[]{:S(2)}) %collective-permute-start.14) | collective-permute-done | bytes 393248 | tf_op jit(solution)/shard_map/ppermute | solution.py:414
  58.0 2.1 %collective-permute-start.5 = (bf16[19,128,128]{2,1,0:T(8,128)(2,1)}, bf16[19,128,128]{2,1,0:T(8,128)(2,1)}, u32[]{:S(2)}, u32[]{:S(2)}) collective-permute-start(bf16[19,128,128]{2,1,0:T(8,128)(2,1)} %get-tuple-element.38), channel_id=1, source_target_pairs={{8,16},{16,8},{24,0},{9,17},{17,9},{25,1},{10,18},{18,10},{26,2},{... | collective-permute-start | bytes 1867784 | tf_op jit(solution)/shard_map/ppermute | solution.py:445
  64.5 2.2 %shard_map.69 = (bf16[6,128,128]{2,1,0:T(8,128)(2,1)S(1)}, bf16[7,128,512]{2,1,0:T(8,128)(2,1)S(1)}, bf16[512,512]{1,0:T(8,128)(2,1)S(1)}) custom-call(s32[5,16]{1,0:T(8,128)S(1)} %copy-done.6, f32[64,128]{1,0:T(8,128)S(1)} %shard_map.64.mask, bf16[19,128,128]{2,1,0:T(8,128)(2,1)S(1)} %copy-done, bf16[19,128,128]{2,1,0:T(8,128)(2,1)S(1)} %collective-permute-done.refs_1_, ...), custom_call_target="tpu_custom_call" | custom-call | flops 100000000 | bytes 1000000 | tf_op jit(solution)/shard_map/pallas_call | solution.py:77
  67.7 3.6 %shard_map.71.own_ref = f32[2,64,128,128]{3,2,1,0:T(8,128)S(1)} custom-call(bf16[6,128,128]{2,1,0:T(8,128)(2,1)S(1)} %get-tuple-element.48.mps_ref, bf16[512,512]{1,0:T(8,128)(2,1)S(1)} %get-tuple-element.50.kron, bf16[2,3,2,128,128]{4,3,2,1,0:T(8,128)(2,1)S(1)} %copy-done.2, bf16[2,3,2,128,128]{4,3,2,1,0:T(8,128)(2,1)} %collective-permute-done.9.refs_1_, ...), custom_call_target="tpu_custom_call" | custom-call | flops 100000000 | bytes 1000000 | tf_op jit(solution)/shard_map/pallas_call | solution.py:77
  71.4 5.1 %shard_map.72 = (bf16[16,2,128,128]{3,2,1,0:T(8,128)(2,1)S(1)}, bf16[4,2,128,128]{3,2,1,0:T(8,128)(2,1)S(1)}) custom-call(s32[16,2]{1,0:T(8,128)S(1)} %copy.12.charges, bf16[6,128,128]{2,1,0:T(8,128)(2,1)S(1)} %get-tuple-element.48.mps_ref, bf16[7,128,512]{2,1,0:T(8,128)(2,1)S(1)} %get-tuple-element.49.turned, bf16[512,512]{1,0:T(8,128)(2,1)S(1)} %get-tuple-element.50.kron, ...), custom_call_target="tpu_custom_call" | custom-call | flops 100000000 | bytes 1000000 | tf_op jit(solution)/shard_map/pallas_call | solution.py:77
  76.4 1.3 collective-permute-start.16
  78.9 2.9 %collective-permute-done.6.refs_7_ = bf16[19,128,128]{2,1,0:T(8,128)(2,1)S(1)} collective-permute-done((bf16[19,128,128]{2,1,0:T(8,128)(2,1)}, bf16[19,128,128]{2,1,0:T(8,128)(2,1)S(1)}, u32[]{:S(2)}, u32[]{:S(2)}) %collective-permute-start.6) | collective-permute-done | bytes 622624 | tf_op jit(solution)/shard_map/ppermute | solution.py:452
  81.9 1.6 %shard_map.68 = (bf16[6,128,128]{2,1,0:T(8,128)(2,1)S(1)}, bf16[7,128,512]{2,1,0:T(8,128)(2,1)S(1)}, bf16[512,512]{1,0:T(8,128)(2,1)S(1)}) custom-call(s32[5,16]{1,0:T(8,128)S(1)} %copy-done.7, f32[64,128]{1,0:T(8,128)S(1)} %shard_map.64.mask, bf16[19,128,128]{2,1,0:T(8,128)(2,1)S(1)} %copy-done.1, bf16[19,128,128]{2,1,0:T(8,128)(2,1)S(1)} %collective-permute-done.refs_1_, ...), custom_call_target="tpu_custom_call" | custom-call | flops 100000000 | bytes 1000000 | tf_op jit(solution)/shard_map/pallas_call | solution.py:77
  83.5 2.2 %shard_map.73.own_ref = f32[2,64,128,128]{3,2,1,0:T(8,128)S(1)} custom-call(bf16[6,128,128]{2,1,0:T(8,128)(2,1)S(1)} %get-tuple-element.45.mps_ref, bf16[512,512]{1,0:T(8,128)(2,1)S(1)} %get-tuple-element.47.kron, bf16[16,2,128,128]{3,2,1,0:T(8,128)(2,1)S(1)} %get-tuple-element.51.refs_0_), custom_call_target="tpu_custom_call" | custom-call | flops 100000000 | bytes 1000000 | tf_op jit(solution)/shard_map/pallas_call | solution.py:77
  85.7 4.2 %shard_map.74 = (bf16[16,2,128,128]{3,2,1,0:T(8,128)(2,1)S(1)}, bf16[4,2,128,128]{3,2,1,0:T(8,128)(2,1)S(1)}) custom-call(s32[16,2]{1,0:T(8,128)S(1)} %copy.12.charges, bf16[6,128,128]{2,1,0:T(8,128)(2,1)S(1)} %get-tuple-element.45.mps_ref, bf16[7,128,512]{2,1,0:T(8,128)(2,1)S(1)} %get-tuple-element.46.turned, bf16[512,512]{1,0:T(8,128)(2,1)S(1)} %get-tuple-element.47.kron, ...), custom_call_target="tpu_custom_call" | custom-call | flops 100000000 | bytes 1000000 | tf_op jit(solution)/shard_map/pallas_call | solution.py:77
  89.9 1.3 collective-permute-start.17
  91.2 1.4 shard_map.67
  92.6 2.2 %shard_map.75.own_ref = f32[2,64,128,128]{3,2,1,0:T(8,128)S(1)} custom-call(bf16[6,128,128]{2,1,0:T(8,128)(2,1)S(1)} %get-tuple-element.42.mps_ref, bf16[512,512]{1,0:T(8,128)(2,1)S(1)} %get-tuple-element.44.kron, bf16[16,2,128,128]{3,2,1,0:T(8,128)(2,1)S(1)} %get-tuple-element.52.refs_0_), custom_call_target="tpu_custom_call" | custom-call | flops 100000000 | bytes 1000000 | tf_op jit(solution)/shard_map/pallas_call | solution.py:77
  94.8 6.4 %collective-permute-done.17.refs_0_ = bf16[16,2,128,128]{3,2,1,0:T(8,128)(2,1)S(1)} collective-permute-done((bf16[16,2,128,128]{3,2,1,0:T(8,128)(2,1)S(1)}, bf16[16,2,128,128]{3,2,1,0:T(8,128)(2,1)S(1)}, u32[]{:S(2)}, u32[]{:S(2)}) %collective-permute-start.17) | collective-permute-done | bytes 1048608 | tf_op jit(solution)/shard_map/ppermute | solution.py:521
  101.2 4.2 %shard_map.76 = (bf16[16,2,128,128]{3,2,1,0:T(8,128)(2,1)S(1)}, bf16[4,2,128,128]{3,2,1,0:T(8,128)(2,1)S(1)}) custom-call(s32[16,2]{1,0:T(8,128)S(1)} %copy.12.charges, bf16[6,128,128]{2,1,0:T(8,128)(2,1)S(1)} %get-tuple-element.42.mps_ref, bf16[7,128,512]{2,1,0:T(8,128)(2,1)S(1)} %get-tuple-element.43.turned, bf16[512,512]{1,0:T(8,128)(2,1)S(1)} %get-tuple-element.44.kron, ...), custom_call_target="tpu_custom_call" | custom-call | flops 100000000 | bytes 1000000 | tf_op jit(solution)/shard_map/pallas_call | solution.py:77
  106.7 1.7 %shard_map.66 = (bf16[6,128,128]{2,1,0:T(8,128)(2,1)S(1)}, bf16[7,128,512]{2,1,0:T(8,128)(2,1)S(1)}, bf16[512,512]{1,0:T(8,128)(2,1)S(1)}) custom-call(s32[5,16]{1,0:T(8,128)S(1)} %copy-done.7, f32[64,128]{1,0:T(8,128)S(1)} %shard_map.64.mask, bf16[19,128,128]{2,1,0:T(8,128)(2,1)S(1)} %copy-done.1, bf16[19,128,128]{2,1,0:T(8,128)(2,1)S(1)} %collective-permute-done.refs_1_, ...), custom_call_target="tpu_custom_call" | custom-call | flops 100000000 | bytes 1000000 | tf_op jit(solution)/shard_map/pallas_call | solution.py:77
  108.4 1.3 shard_map.77.own_ref
  109.7 11.8 %collective-permute-done.18.refs_0_ = bf16[16,2,128,128]{3,2,1,0:T(8,128)(2,1)S(1)} collective-permute-done((bf16[16,2,128,128]{3,2,1,0:T(8,128)(2,1)S(1)}, bf16[16,2,128,128]{3,2,1,0:T(8,128)(2,1)S(1)}, u32[]{:S(2)}, u32[]{:S(2)}) %collective-permute-start.18) | collective-permute-done | bytes 1048608 | tf_op jit(solution)/shard_map/ppermute | solution.py:521
  121.5 2.7 %shard_map.78 = (bf16[2,2,128,128]{3,2,1,0:T(8,128)(2,1)S(1)}, bf16[2,2,128,128]{3,2,1,0:T(8,128)(2,1)S(1)}, bf16[2,2,128,128]{3,2,1,0:T(8,128)(2,1)S(1)}, bf16[...) custom-call(s32[16,2]{1,0:T(8,128)S(1)} %copy.12.charges, ...), custom_call_target="tpu_custom_call" | custom-call | flops 100000000 | bytes 1000000 | tf_op jit(solution)/shard_map/pallas_call | solution.py:77
  124.3 12.1 %collective-permute-start.19 = (bf16[2,2,128,128]{3,2,1,0:T(8,128)(2,1)S(1)}, bf16[2,2,128,128]{3,2,1,0:T(8,128)(2,1)S(1)}, u32[]{:S(2)}, u32[]{:S(2)}) collective-permute-start(bf16[2,2,128,128]{3,2,1,0:T(8,128)(2,1)S(1)} %get-tuple-element.58), channel_id=1, source_target_pairs={{0,1},{1,0},{2,3},{3,2},{4,5},{5,4},{6,7},{7,6},{8,9},{9,8},{10,11... | collective-permute-start | bytes 393224 | tf_op jit(solution)/shard_map/ppermute | solution.py:528
  136.4 1.7 %collective-permute-start.21 = (bf16[2,2,128,128]{3,2,1,0:T(8,128)(2,1)S(1)}, bf16[2,2,128,128]{3,2,1,0:T(8,128)(2,1)S(1)}, u32[]{:S(2)}, u32[]{:S(2)}) collective-permute-start(bf16[2,2,128,128]{3,2,1,0:T(8,128)(2,1)S(1)} %get-tuple-element.60), channel_id=1, source_target_pairs={{0,9},{1,8},{2,11},{3,10},{4,13},{5,12},{6,15},{7,14},{8,1},{9,0},... | collective-permute-start | bytes 393224 | tf_op jit(solution)/shard_map/ppermute | solution.py:528
  138.1 1.8 %collective-permute-start.23 = (bf16[2,2,128,128]{3,2,1,0:T(8,128)(2,1)S(1)}, bf16[2,2,128,128]{3,2,1,0:T(8,128)(2,1)S(1)}, u32[]{:S(2)}, u32[]{:S(2)}) collective-permute-start(bf16[2,2,128,128]{3,2,1,0:T(8,128)(2,1)S(1)} %get-tuple-element.62), channel_id=1, source_target_pairs={{0,17},{1,16},{2,19},{3,18},{4,21},{5,20},{6,23},{7,22},{8,25},{9,... | collective-permute-start | bytes 393224 | tf_op jit(solution)/shard_map/ppermute | solution.py:528
  139.9 1.5 collective-permute-done.20.refs_2_
  142.5 2.8 %collective-permute-done.21.refs_3_ = bf16[2,2,128,128]{3,2,1,0:T(8,128)(2,1)S(1)} collective-permute-done((bf16[2,2,128,128]{3,2,1,0:T(8,128)(2,1)S(1)}, bf16[2,2,128,128]{3,2,1,0:T(8,128)(2,1)S(1)}, u32[]{:S(2)}, u32[]{:S(2)}) %collective-permute-start.21) | collective-permute-done | bytes 131104 | tf_op jit(solution)/shard_map/ppermute | solution.py:528
  145.3 6.5 %collective-permute-done.23.refs_5_ = bf16[2,2,128,128]{3,2,1,0:T(8,128)(2,1)S(1)} collective-permute-done((bf16[2,2,128,128]{3,2,1,0:T(8,128)(2,1)S(1)}, bf16[2,2,128,128]{3,2,1,0:T(8,128)(2,1)S(1)}, u32[]{:S(2)}, u32[]{:S(2)}) %collective-permute-start.23) | collective-permute-done | bytes 131104 | tf_op jit(solution)/shard_map/ppermute | solution.py:528
  (58 shorter events, 16.4 us)
Async XLA Ops:
  5.9 21.7 %collective-permute-start.1 = (bf16[19,128,128]{2,1,0:T(8,128)(2,1)}, bf16[19,128,128]{2,1,0:T(8,128)(2,1)S(1)}, u32[]{:S(2)}, u32[]{:S(2)}) collective-permute-start(bf16[19,128,128]{2,1,0:T(8,128)(2,1)} %get-tuple-element.36), channel_id=1, source_target_pairs={{0,8},{8,0},{16,24},{24,16},{1,9},{9,1},{17,25},{25,17},{2,10},{10... | collective-permute-start | bytes 1867784 | tf_op jit(solution)/shard_map/ppermute | solution.py:441
  6.2 21.4 %collective-permute-start.3 = (bf16[19,128,128]{2,1,0:T(8,128)(2,1)}, bf16[19,128,128]{2,1,0:T(8,128)(2,1)S(1)}, u32[]{:S(2)}, u32[]{:S(2)}) collective-permute-start(bf16[19,128,128]{2,1,0:T(8,128)(2,1)} %get-tuple-element.37), channel_id=1, source_target_pairs={{0,16},{8,24},{16,0},{24,8},{1,17},{9,25},{17,1},{25,9},{2,18},{10... | collective-permute-start | bytes 1867784 | tf_op jit(solution)/shard_map/ppermute | solution.py:441
  6.5 29.8 %collective-permute-start.7 = (bf16[19,128,128]{2,1,0:T(8,128)(2,1)}, bf16[19,128,128]{2,1,0:T(8,128)(2,1)}, u32[]{:S(2)}, u32[]{:S(2)}) collective-permute-start(bf16[19,128,128]{2,1,0:T(8,128)(2,1)} %get-tuple-element.38), channel_id=1, source_target_pairs={{0,24},{1,25},{2,26},{3,27},{4,28},{5,29},{6,30},{7,31}} | collective-permute-start | bytes 1867784 | tf_op jit(solution)/shard_map/ppermute | solution.py:443
  9.6 16.2 %collective-permute-start.10 = (bf16[2,3,2,128,128]{4,3,2,1,0:T(8,128)(2,1)}, bf16[2,3,2,128,128]{4,3,2,1,0:T(8,128)(2,1)S(1)}, u32[]{:S(2)}, u32[]{:S(2)}) collective-permute-start(bf16[2,3,2,128,128]{4,3,2,1,0:T(8,128)(2,1)} %shard_map.70.refs_0_), channel_id=1, source_target_pairs={{0,2},{1,3},{2,0},{3,1},{4,6},{5,7},{6,4},{7,5},{8,10},{9,11},{10,... | collective-permute-start | bytes 1179656 | tf_op jit(solution)/shard_map/ppermute | solution.py:414
  9.7 26.6 %collective-permute-start.12 = (bf16[2,3,2,128,128]{4,3,2,1,0:T(8,128)(2,1)}, bf16[2,3,2,128,128]{4,3,2,1,0:T(8,128)(2,1)}, u32[]{:S(2)}, u32[]{:S(2)}) collective-permute-start(bf16[2,3,2,128,128]{4,3,2,1,0:T(8,128)(2,1)} %shard_map.70.refs_0_), channel_id=1, source_target_pairs={{0,4},{1,5},{2,6},{3,7},{4,0},{5,1},{6,2},{7,3},{8,12},{9,13},{10,... | collective-permute-start | bytes 1179656 | tf_op jit(solution)/shard_map/ppermute | solution.py:414
  25.8 30.8 %collective-permute-start = (bf16[19,128,128]{2,1,0:T(8,128)(2,1)}, bf16[19,128,128]{2,1,0:T(8,128)(2,1)S(1)}, u32[]{:S(2)}, u32[]{:S(2)}) collective-permute-start(bf16[19,128,128]{2,1,0:T(8,128)(2,1)} %get-tuple-element.35.refs_0_), channel_id=1, source_target_pairs={{0,1},{1,0},{2,3},{3,2},{4,5},{5,4},{6,7},{7,6},{8,9},{9,8},{10,11... | collective-permute-start | bytes 1867784 | tf_op jit(solution)/shard_map/ppermute | solution.py:452
  27.6 29.0 %collective-permute-start.2 = (bf16[19,128,128]{2,1,0:T(8,128)(2,1)S(1)}, bf16[19,128,128]{2,1,0:T(8,128)(2,1)S(1)}, u32[]{:S(2)}, u32[]{:S(2)}) collective-permute-start(bf16[19,128,128]{2,1,0:T(8,128)(2,1)S(1)} %collective-permute-done.1.refs_2_), channel_id=1, source_target_pairs={{0,1},{1,0},{2,3},{3,2},{4,5},{5,4},{6,7},{7,6},{8,9},{9,8},{10,11... | collective-permute-start | bytes 1867784 | tf_op jit(solution)/shard_map/ppermute | solution.py:452
  27.6 29.5 %collective-permute-start.4 = (bf16[19,128,128]{2,1,0:T(8,128)(2,1)S(1)}, bf16[19,128,128]{2,1,0:T(8,128)(2,1)S(1)}, u32[]{:S(2)}, u32[]{:S(2)}) collective-permute-start(bf16[19,128,128]{2,1,0:T(8,128)(2,1)S(1)} %collective-permute-done.3.refs_4_), channel_id=1, source_target_pairs={{0,1},{1,0},{2,3},{3,2},{4,5},{5,4},{6,7},{7,6},{8,9},{9,8},{10,11... | collective-permute-start | bytes 1867784 | tf_op jit(solution)/shard_map/ppermute | solution.py:452
  36.2 20.9 %collective-permute-start.8 = (bf16[19,128,128]{2,1,0:T(8,128)(2,1)}, bf16[19,128,128]{2,1,0:T(8,128)(2,1)S(1)}, u32[]{:S(2)}, u32[]{:S(2)}) collective-permute-start(bf16[19,128,128]{2,1,0:T(8,128)(2,1)} %collective-permute-done.7.refs_6_), channel_id=1, source_target_pairs={{0,1},{1,0},{2,3},{3,2},{4,5},{5,4},{6,7},{7,6},{8,9},{9,8},{10,11... | collective-permute-start | bytes 1867784 | tf_op jit(solution)/shard_map/ppermute | solution.py:452
  36.3 19.0 %collective-permute-start.14 = (bf16[2,3,2,128,128]{4,3,2,1,0:T(8,128)(2,1)}, bf16[2,3,2,128,128]{4,3,2,1,0:T(8,128)(2,1)}, u32[]{:S(2)}, u32[]{:S(2)}) collective-permute-start(bf16[2,3,2,128,128]{4,3,2,1,0:T(8,128)(2,1)} %shard_map.70.refs_0_), channel_id=1, source_target_pairs={{0,6},{1,7},{2,4},{3,5},{4,2},{5,3},{6,0},{7,1},{8,14},{9,15},{10,... | collective-permute-start | bytes 1179656 | tf_op jit(solution)/shard_map/ppermute | solution.py:414
  55.3 11.4 %collective-permute-start.9 = (bf16[2,3,2,128,128]{4,3,2,1,0:T(8,128)(2,1)}, bf16[2,3,2,128,128]{4,3,2,1,0:T(8,128)(2,1)}, u32[]{:S(2)}, u32[]{:S(2)}) collective-permute-start(bf16[2,3,2,128,128]{4,3,2,1,0:T(8,128)(2,1)} %shard_map.70.refs_0_), channel_id=1, source_target_pairs={{0,1},{1,0},{2,3},{3,2},{4,5},{5,4},{6,7},{7,6},{8,9},{9,8},{10,11... | collective-permute-start | bytes 1179656 | tf_op jit(solution)/shard_map/ppermute | solution.py:419
  56.6 10.1 %collective-permute-start.11 = (bf16[2,3,2,128,128]{4,3,2,1,0:T(8,128)(2,1)S(1)}, bf16[2,3,2,128,128]{4,3,2,1,0:T(8,128)(2,1)}, u32[]{:S(2)}, u32[]{:S(2)}) collective-permute-start(bf16[2,3,2,128,128]{4,3,2,1,0:T(8,128)(2,1)S(1)} %collective-permute-done.10.refs_2_), channel_id=1, source_target_pairs={{0,1},{1,0},{2,3},{3,2},{4,5},{5,4},{6,7},{7,6},{8,9},{9,8},{10,11... | collective-permute-start | bytes 1179656 | tf_op jit(solution)/shard_map/ppermute | solution.py:419
  56.6 10.1 %collective-permute-start.13 = (bf16[2,3,2,128,128]{4,3,2,1,0:T(8,128)(2,1)}, bf16[2,3,2,128,128]{4,3,2,1,0:T(8,128)(2,1)}, u32[]{:S(2)}, u32[]{:S(2)}) collective-permute-start(bf16[2,3,2,128,128]{4,3,2,1,0:T(8,128)(2,1)} %collective-permute-done.12.refs_4_), channel_id=1, source_target_pairs={{0,1},{1,0},{2,3},{3,2},{4,5},{5,4},{6,7},{7,6},{8,9},{9,8},{10,11... | collective-permute-start | bytes 1179656 | tf_op jit(solution)/shard_map/ppermute | solution.py:419
  57.1 9.6 %collective-permute-start.15 = (bf16[2,3,2,128,128]{4,3,2,1,0:T(8,128)(2,1)}, bf16[2,3,2,128,128]{4,3,2,1,0:T(8,128)(2,1)}, u32[]{:S(2)}, u32[]{:S(2)}) collective-permute-start(bf16[2,3,2,128,128]{4,3,2,1,0:T(8,128)(2,1)} %collective-permute-done.14.refs_6_), channel_id=1, source_target_pairs={{0,1},{1,0},{2,3},{3,2},{4,5},{5,4},{6,7},{7,6},{8,9},{9,8},{10,11... | collective-permute-start | bytes 1179656 | tf_op jit(solution)/shard_map/ppermute | solution.py:419
  58.0 19.7 %collective-permute-start.5 = (bf16[19,128,128]{2,1,0:T(8,128)(2,1)}, bf16[19,128,128]{2,1,0:T(8,128)(2,1)}, u32[]{:S(2)}, u32[]{:S(2)}) collective-permute-start(bf16[19,128,128]{2,1,0:T(8,128)(2,1)} %get-tuple-element.38), channel_id=1, source_target_pairs={{8,16},{16,8},{24,0},{9,17},{17,9},{25,1},{10,18},{18,10},{26,2},{... | collective-permute-start | bytes 1867784 | tf_op jit(solution)/shard_map/ppermute | solution.py:445
  61.6 1.1 copy-start
  62.7 1.1 copy-start.5
  64.5 6.9 %copy-start.3 = (bf16[2,3,2,128,128]{4,3,2,1,0:T(8,128)(2,1)S(1)}, bf16[2,3,2,128,128]{4,3,2,1,0:T(8,128)(2,1)}, u32[]{:S(2)}) copy-start(bf16[2,3,2,128,128]{4,3,2,1,0:T(8,128)(2,1)} %shard_map.70.refs_0_) | copy-start | bytes 1179652
  66.7 1.0 copy-start.2
  71.3 10.6 %copy-start.1 = (bf16[19,128,128]{2,1,0:T(8,128)(2,1)S(1)}, bf16[19,128,128]{2,1,0:T(8,128)(2,1)}, u32[]{:S(2)}) copy-start(bf16[19,128,128]{2,1,0:T(8,128)(2,1)} %get-tuple-element.35.refs_0_) | copy-start | bytes 1867780
  71.3 10.6 %copy-start.7 = (s32[5,16]{1,0:T(8,128)S(1)}, s32[5,16]{1,0:T(8,128)}, u32[]{:S(2)}) copy-start(s32[5,16]{1,0:T(8,128)} %sizes.7) | copy-start | bytes 964
  76.4 9.2 %collective-permute-start.16 = (bf16[16,2,128,128]{3,2,1,0:T(8,128)(2,1)S(1)}, bf16[16,2,128,128]{3,2,1,0:T(8,128)(2,1)S(1)}, u32[]{:S(2)}, u32[]{:S(2)}) collective-permute-start(bf16[16,2,128,128]{3,2,1,0:T(8,128)(2,1)S(1)} %get-tuple-element.51.refs_0_), channel_id=1, source_target_pairs={{0,1},{1,8},{2,3},{3,10},{4,5},{5,12},{6,7},{7,14},{8,9},{9,24},{1... | collective-permute-start | bytes 3145736 | tf_op jit(solution)/shard_map/ppermute | solution.py:521
  77.8 4.1 %collective-permute-start.6 = (bf16[19,128,128]{2,1,0:T(8,128)(2,1)}, bf16[19,128,128]{2,1,0:T(8,128)(2,1)S(1)}, u32[]{:S(2)}, u32[]{:S(2)}) collective-permute-start(bf16[19,128,128]{2,1,0:T(8,128)(2,1)} %collective-permute-done.5.refs_6_), channel_id=1, source_target_pairs={{0,1},{1,0},{2,3},{3,2},{4,5},{5,4},{6,7},{7,6},{8,9},{9,8},{10,11... | collective-permute-start | bytes 1867784 | tf_op jit(solution)/shard_map/ppermute | solution.py:452
  89.9 11.4 %collective-permute-start.17 = (bf16[16,2,128,128]{3,2,1,0:T(8,128)(2,1)S(1)}, bf16[16,2,128,128]{3,2,1,0:T(8,128)(2,1)S(1)}, u32[]{:S(2)}, u32[]{:S(2)}) collective-permute-start(bf16[16,2,128,128]{3,2,1,0:T(8,128)(2,1)S(1)} %get-tuple-element.52.refs_0_), channel_id=1, source_target_pairs={{0,1},{1,8},{2,3},{3,10},{4,5},{5,12},{6,7},{7,14},{8,9},{9,24},{1... | collective-permute-start | bytes 3145736 | tf_op jit(solution)/shard_map/ppermute | solution.py:521
  105.4 16.1 %collective-permute-start.18 = (bf16[16,2,128,128]{3,2,1,0:T(8,128)(2,1)S(1)}, bf16[16,2,128,128]{3,2,1,0:T(8,128)(2,1)S(1)}, u32[]{:S(2)}, u32[]{:S(2)}) collective-permute-start(bf16[16,2,128,128]{3,2,1,0:T(8,128)(2,1)S(1)} %get-tuple-element.53.refs_0_), channel_id=1, source_target_pairs={{0,1},{1,8},{2,3},{3,10},{4,5},{5,12},{6,7},{7,14},{8,9},{9,24},{1... | collective-permute-start | bytes 3145736 | tf_op jit(solution)/shard_map/ppermute | solution.py:521
  124.3 15.6 %collective-permute-start.19 = (bf16[2,2,128,128]{3,2,1,0:T(8,128)(2,1)S(1)}, bf16[2,2,128,128]{3,2,1,0:T(8,128)(2,1)S(1)}, u32[]{:S(2)}, u32[]{:S(2)}) collective-permute-start(bf16[2,2,128,128]{3,2,1,0:T(8,128)(2,1)S(1)} %get-tuple-element.58), channel_id=1, source_target_pairs={{0,1},{1,0},{2,3},{3,2},{4,5},{5,4},{6,7},{7,6},{8,9},{9,8},{10,11... | collective-permute-start | bytes 393224 | tf_op jit(solution)/shard_map/ppermute | solution.py:528
  136.4 5.0 %collective-permute-start.20 = (bf16[2,2,128,128]{3,2,1,0:T(8,128)(2,1)S(1)}, bf16[2,2,128,128]{3,2,1,0:T(8,128)(2,1)S(1)}, u32[]{:S(2)}, u32[]{:S(2)}) collective-permute-start(bf16[2,2,128,128]{3,2,1,0:T(8,128)(2,1)S(1)} %get-tuple-element.59), channel_id=1, source_target_pairs={{0,8},{1,9},{2,10},{3,11},{4,12},{5,13},{6,14},{7,15},{8,0},{9,1},... | collective-permute-start | bytes 393224 | tf_op jit(solution)/shard_map/ppermute | solution.py:528
  136.4 8.9 %collective-permute-start.21 = (bf16[2,2,128,128]{3,2,1,0:T(8,128)(2,1)S(1)}, bf16[2,2,128,128]{3,2,1,0:T(8,128)(2,1)S(1)}, u32[]{:S(2)}, u32[]{:S(2)}) collective-permute-start(bf16[2,2,128,128]{3,2,1,0:T(8,128)(2,1)S(1)} %get-tuple-element.60), channel_id=1, source_target_pairs={{0,9},{1,8},{2,11},{3,10},{4,13},{5,12},{6,15},{7,14},{8,1},{9,0},... | collective-permute-start | bytes 393224 | tf_op jit(solution)/shard_map/ppermute | solution.py:528
  138.1 7.2 %collective-permute-start.22 = (bf16[2,2,128,128]{3,2,1,0:T(8,128)(2,1)S(1)}, bf16[2,2,128,128]{3,2,1,0:T(8,128)(2,1)S(1)}, u32[]{:S(2)}, u32[]{:S(2)}) collective-permute-start(bf16[2,2,128,128]{3,2,1,0:T(8,128)(2,1)S(1)} %get-tuple-element.61), channel_id=1, source_target_pairs={{0,16},{1,17},{2,18},{3,19},{4,20},{5,21},{6,22},{7,23},{8,24},{9,... | collective-permute-start | bytes 393224 | tf_op jit(solution)/shard_map/ppermute | solution.py:528
  138.1 13.6 %collective-permute-start.23 = (bf16[2,2,128,128]{3,2,1,0:T(8,128)(2,1)S(1)}, bf16[2,2,128,128]{3,2,1,0:T(8,128)(2,1)S(1)}, u32[]{:S(2)}, u32[]{:S(2)}) collective-permute-start(bf16[2,2,128,128]{3,2,1,0:T(8,128)(2,1)S(1)} %get-tuple-element.62), channel_id=1, source_target_pairs={{0,17},{1,16},{2,19},{3,18},{4,21},{5,20},{6,23},{7,22},{8,25},{9,... | collective-permute-start | bytes 393224 | tf_op jit(solution)/shard_map/ppermute | solution.py:528
  139.9 11.9 %collective-permute-start.24 = (bf16[2,2,128,128]{3,2,1,0:T(8,128)(2,1)S(1)}, bf16[2,2,128,128]{3,2,1,0:T(8,128)(2,1)S(1)}, u32[]{:S(2)}, u32[]{:S(2)}) collective-permute-start(bf16[2,2,128,128]{3,2,1,0:T(8,128)(2,1)S(1)} %get-tuple-element.63), channel_id=1, source_target_pairs={{0,24},{1,25},{2,26},{3,27},{4,28},{5,29},{6,30},{7,31},{8,16},{9,... | collective-permute-start | bytes 393224 | tf_op jit(solution)/shard_map/ppermute | solution.py:528
  141.4 10.4 %collective-permute-start.25 = (bf16[2,2,128,128]{3,2,1,0:T(8,128)(2,1)S(1)}, bf16[2,2,128,128]{3,2,1,0:T(8,128)(2,1)S(1)}, u32[]{:S(2)}, u32[]{:S(2)}) collective-permute-start(bf16[2,2,128,128]{3,2,1,0:T(8,128)(2,1)S(1)} %get-tuple-element.64), channel_id=1, source_target_pairs={{0,25},{1,24},{2,27},{3,26},{4,29},{5,28},{6,31},{7,30},{8,17},{9,... | collective-permute-start | bytes 393224 | tf_op jit(solution)/shard_map/ppermute | solution.py:528
  (2 other events, 1.5 us)

commit v2 on v1

v2 whole, which is shorter than its diff:
```python
import functools

import jax
import jax.numpy as jnp
from jax import lax
from jax.experimental import pallas as pl
from jax.experimental.pallas import tpu as pltpu
from jax.sharding import PartitionSpec as P


UP_VALUES = 8
DOWN_VALUES = 2
PHYS = 4

UP_CHARGE = (0, 1, 0, 1)
DOWN_CHARGE = (0, 0, 1, 1)

STATE_ORDER = (0, 2, 1, 3)
MPS_PARTS = ((0, 0, 2), (2, 0, 1), (1, -1, 2), (3, -1, 1))
MPS_BLOCKS = ((0, 0, 0), (0, 0, 1), (2, 0, 0), (1, -1, 0), (1, -1, 1), (3, -1, 0))
ROW_SHIFTS = 3
PROJ_PARTS = ((0, -1, 2), (1, -2, 2), (2, -1, 1), (3, -2, 1))
GROUP = 8


VMEM = pl.BlockSpec(memory_space=pltpu.VMEM)
SMEM = pl.BlockSpec(memory_space=pltpu.SMEM)
ANY = pl.BlockSpec(memory_space=pl.ANY)
HBM = pl.BlockSpec(memory_space=pltpu.HBM)


def ring_chain(position, count):
    turned = (position + count - 1) % count
    return turned ^ (turned >> 1)


def place(chain, count):
    plain = chain ^ (chain >> 1) ^ (chain >> 2)
    return (plain + 1) % count if isinstance(chain, int) else lax.rem(plain + 1, count)


def my_row(chain_count, spread):
    side = lax.rem(lax.axis_index("op"), spread)
    return place(lax.axis_index("chain"), chain_count) * spread + side


def held_rows(spread):
    return -(-(ROW_SHIFTS + spread - 1) // spread)


def held_base(first_row, offset, holder, spread):
    rows = held_rows(spread)
    return jnp.clip(first_row + offset + holder * rows, 0, UP_VALUES - rows)


def proj_start(phys_state, spread):
    start = len(MPS_BLOCKS)
    for part_state, _, downs in PROJ_PARTS:
        if part_state == phys_state:
            return start
        start += held_rows(spread) * downs
    return start


def mpo_matrix(site_mpo):
    bond = site_mpo.shape[0]
    ordered = jnp.stack([site_mpo[:, state] for state in STATE_ORDER], axis=1)
    return jnp.transpose(ordered, (2, 3, 1, 0)).reshape(bond * PHYS, PHYS * bond)


def call(kernel, *args, **options):
    return plain_call(kernel, *args, **options)


def plain_call(kernel, out_shape, specs, operands, scratch=(), limit=20, flops=10**8, place_out=VMEM):
    one = not isinstance(out_shape, (list, tuple))
    return pl.pallas_call(
        kernel,
        out_shape=out_shape,
        in_specs=specs,
        out_specs=place_out if one else tuple(place_out for _ in out_shape),
        scratch_shapes=list(scratch),
        compiler_params=pltpu.CompilerParams(vmem_limit_bytes=limit << 20),
        cost_estimate=pl.CostEstimate(flops=flops, bytes_accessed=10**6, transcendentals=0),
    )(*operands)


def shape_of(*dims, dtype=jnp.bfloat16):
    return jax.ShapeDtypeStruct(dims, dtype)


def run_copies(copies):
    for copy in copies:
        copy.start()
    for copy in copies:
        copy.wait()


def pack_env_kernel(chain_count, spread, env_ref, out_ref, sem):
    first = place(lax.axis_index("chain"), chain_count) * spread
    before = jnp.maximum(first - 1, 0)
    copies = []

    def add(source, target):
        copies.append(pltpu.make_async_copy(source, target, sem.at[len(copies)]))

    for bond in range(env_ref.shape[0]):
        add(env_ref.at[bond, pl.ds(before, 1)], out_ref.at[bond, pl.ds(0, 1)])
        add(env_ref.at[bond, pl.ds(first, spread)], out_ref.at[bond, pl.ds(1, spread)])
    run_copies(copies)


def pack_site_kernel(chain_count, spread, first_hop, mps_ref, proj_ref, *refs):
    out_refs, sem = refs[:-1], refs[-1]
    chain_pos = lax.axis_index("chain")
    side = lax.rem(lax.axis_index("op"), spread)
    is_last = (chain_pos == chain_count - 1).astype(jnp.int32)
    copies = []

    def add(source, target):
        copies.append(pltpu.make_async_copy(source, target, sem.at[len(copies)]))

    rows = held_rows(spread)
    for hop, out_ref in enumerate(out_refs, first_hop):
        first = place(jnp.bitwise_xor(chain_pos, hop), chain_count) * spread
        start = 0
        for phys_state, offset, downs in MPS_PARTS:
            late = is_last if offset else 0
            sector = jnp.maximum(first + side + offset + late, 0) * DOWN_VALUES
            add(
                mps_ref.at[0, phys_state, pl.ds(sector, downs)],
                out_ref.at[pl.ds(start, downs)],
            )
            start += downs
        for phys_state, offset, downs in PROJ_PARTS:
            base = held_base(first, offset, side, spread)
            start = proj_start(phys_state, spread)
            for down in range(downs):
                add(
                    proj_ref.at[0, phys_state, pl.ds(base, rows), down],
                    out_ref.at[pl.ds(start + down * rows, rows)],
                )
    run_copies(copies)


def pack_extra_kernel(chain_count, spread, proj_ref, *refs):
    out_refs, sem = refs[:-1], refs[-1]
    copies = []
    for hop, out_ref in enumerate(out_refs):
        first = place(jnp.bitwise_xor(lax.axis_index("chain"), hop), chain_count) * spread
        start = 0
        for phys_state, offset, downs in PROJ_PARTS:
            at = jnp.minimum(first + offset + spread + ROW_SHIFTS - 1, UP_VALUES - 1)
            copies.append(
                pltpu.make_async_copy(
                    proj_ref.at[0, phys_state, at, pl.ds(0, downs)],
                    out_ref.at[pl.ds(start, downs)],
                    sem.at[len(copies)],
                )
            )
            start += downs
    run_copies(copies)


def mask_kernel(charges, out_ref):
    rows, lanes = out_ref.shape
    bond = rows // PHYS
    row_at = lax.broadcasted_iota(jnp.int32, (rows, lanes), 0)
    lane_at = lax.broadcasted_iota(jnp.int32, (rows, lanes), 1)
    ones = jnp.ones((rows, lanes), jnp.float32)
    for axis, table in enumerate((UP_CHARGE, DOWN_CHARGE)):
        left = jnp.zeros((rows, lanes), jnp.int32)
        right = jnp.zeros((rows, lanes), jnp.int32)
        for index in range(bond):
            value = charges[index, axis]
            left = jnp.where(row_at // PHYS == index, value, left)
            right = jnp.where(lane_at % bond == index, value, right)
        for index in range(PHYS):
            left = left - jnp.where(row_at % PHYS == index, table[index], 0)
            right = right - jnp.where(lane_at // bond == index, table[STATE_ORDER[index]], 0)
        ones = jnp.where(left == right, ones, 0.0)
    out_ref[...] = ones


def turn_blocks(turned, row, side, spread, block, read, read_extra=None):
    held = held_rows(spread)
    turned[...] = jnp.zeros_like(turned)
    extra = 0
    for phys_state, offset, downs in PROJ_PARTS:
        for shift in range(ROW_SHIFTS):
            for target in range(DOWN_VALUES):
                down = target - DOWN_CHARGE[phys_state]
                if down < 0:
                    continue
                wanted = row + offset + shift
                holder = jnp.minimum((side + shift) // held, spread - 1)
                base = held_base(row - side, offset, holder, spread)
                at = jnp.clip(wanted - base, 0, held - 1)
                value = read(holder, proj_start(phys_state, spread) + down * held + at)
                if read_extra is not None and shift == ROW_SHIFTS - 1:
                    beyond = side + shift >= spread + ROW_SHIFTS - 1
                    value = jnp.where(beyond, read_extra(extra + down), value)
                inside = (wanted >= 0) & (wanted < UP_VALUES)
                turned[
                    shift * DOWN_VALUES + target,
                    :,
                    phys_state * block : (phys_state + 1) * block,
                ] = jnp.where(inside, value.T, jnp.zeros_like(value))
        extra += downs


def prep_kernel(site, last, chain_count, spread, bond, block, slots, sizes, mask, *refs):
    matrix_refs, refs = refs[:slots], refs[slots:]
    weight_refs, refs = refs[: slots * spread], refs[slots * spread :]
    extra_refs, refs = (refs[:slots], refs[slots:]) if last else ((), refs)
    mps_ref, turned, kron = refs[:3]
    weights, sem = refs[-2:]
    row = my_row(chain_count, spread)
    side = lax.rem(lax.axis_index("op"), spread)
    slot = jnp.bitwise_xor(lax.axis_index("chain"), site)
    for index in range(slots):
        @pl.when(slot == index)
        def _():
            run_copies(
                [
                    pltpu.make_async_copy(
                        weight_refs[index * spread + turn],
                        weights.at[jnp.bitwise_xor(side, turn)],
                        sem.at[turn],
                    )
                    for turn in range(spread)
                ]
            )

    row_at = lax.broadcasted_iota(jnp.int32, (block, block), 0)
    column_at = lax.broadcasted_iota(jnp.int32, (block, block), 1)
    for index, (phys_state, offset, down) in enumerate(MPS_BLOCKS):
        late = 1 if last and offset else 0
        source = row + offset + late
        target = jnp.minimum(row + late, UP_VALUES - 1)
        high = sizes[site, jnp.maximum(source, 0) * DOWN_VALUES + down]
        wide = sizes[site + 1, target * DOWN_VALUES + down + DOWN_CHARGE[phys_state]]
        keep = (row_at < jnp.where(source >= 0, high, 0)) & (column_at < wide)
        value = weights[side, index]
        mps_ref[index] = jnp.where(keep, value, jnp.zeros_like(value))

    def read(holder, at):
        return weights[holder, at]

    turn_blocks(turned, row, side, spread, block, read)
    if last:

        def read_extra(at):
            value = extra_refs[0][at]
            for index in range(1, slots):
                value = jnp.where(slot == index, extra_refs[index][at], value)
            return value

        turn_blocks(refs[3], row + 1, side + 1, spread, block, read, read_extra)

    pairs = bond * PHYS
    wide = pairs * GROUP
    matrix = matrix_refs[0][...].astype(jnp.float32)
    for index in range(1, slots):
        matrix = jnp.where(slot == index, matrix_refs[index][...].astype(jnp.float32), matrix)
    matrix = jnp.where(mask[...] > 0.5, matrix, 0.0).astype(jnp.bfloat16)
    lanes = matrix.shape[1]
    tall = (
        lax.broadcasted_iota(jnp.int32, (wide, pairs), 0) // GROUP
        == lax.broadcasted_iota(jnp.int32, (wide, pairs), 1)
    ).astype(jnp.bfloat16)
    across = (
        lax.broadcasted_iota(jnp.int32, (lanes, wide), 0)
        == lax.broadcasted_iota(jnp.int32, (lanes, wide), 1) // GROUP
    ).astype(jnp.bfloat16)
    spread_out = jnp.dot(tall, matrix, preferred_element_type=jnp.float32).astype(jnp.bfloat16)
    spread_out = jnp.dot(spread_out, across, preferred_element_type=jnp.float32)
    same = (
        lax.broadcasted_iota(jnp.int32, (wide, wide), 0) % GROUP
        == lax.broadcasted_iota(jnp.int32, (wide, wide), 1) % GROUP
    )
    kron[...] = jnp.where(same, spread_out, 0.0).astype(jnp.bfloat16)


def mix(env_refs, offset, mps_ref, spread, bond, flat, deep, flat_at, deep_at):
    block = mps_ref.shape[-1]
    first_block = 0 if offset == 0 else len(MPS_BLOCKS) // 2
    level, falling = mps_ref[first_block], mps_ref[first_block + 2]
    right = jnp.concatenate([level, falling], axis=1)
    per_chunk = bond // len(env_refs)
    for index, ref in enumerate(env_refs):
        if len(env_refs) == 1:
            first, rows = 0, (ref[:, 0], ref[:, 1])
        else:
            op_pos = lax.axis_index("op")
            first = jnp.bitwise_xor(op_pos, index) * per_chunk
            at = lax.rem(op_pos, spread) + 1 + offset
            rows = (ref[:, at, 0], ref[:, at, 1])
        low, high = (
            jnp.dot(
                part.reshape(per_chunk * block, block), other, preferred_element_type=jnp.float32
            )
            for part, other in zip(rows, (right, mps_ref[first_block + 1]))
        )
        shape = (per_chunk, block, block)
        flat[pl.ds(flat_at + first, per_chunk)] = low[:, :block].reshape(shape)
        deep[pl.ds(deep_at + bond + first, per_chunk)] = low[:, block:].reshape(shape)
        deep[pl.ds(deep_at + first, per_chunk)] = high.reshape(shape)


def contract(mixed, left, store):
    block = mixed.shape[-1]
    rows, columns = left.shape
    used = columns // GROUP

    def body(index, carry):
        at = pl.multiple_of(index * 2 * GROUP, 2 * GROUP)
        low = mixed[:used, pl.ds(at, GROUP), :].reshape(columns, block)
        high = mixed[:used, pl.ds(at + GROUP, GROUP), :].reshape(columns, block)
        right = jnp.concatenate([low, high], axis=1).astype(jnp.bfloat16)
        got = jnp.dot(left, right, preferred_element_type=jnp.float32)
        store(
            at,
            got[:, :block].reshape(rows // GROUP, GROUP, block),
            got[:, block:].reshape(rows // GROUP, GROUP, block),
        )
        return carry

    steps = block // (2 * GROUP)
    lax.fori_loop(0, steps, body, 0, unroll=steps)


def left_rows(pairs, kept_rows, spread):
    if kept_rows == pairs:
        return pl.ds(0, pairs * GROUP)
    layer = lax.axis_index("op") // spread
    return pl.ds(pl.multiple_of(layer * (kept_rows * GROUP), kept_rows * GROUP), kept_rows * GROUP)


def own_kernel(spread, bond, mps_ref, kron, env_ref, out_ref, flat, deep):
    mix([env_ref], 0, mps_ref, spread, bond, flat, deep, 0, 0)
    for down, (mixed, states) in enumerate(((flat, 1), (deep, 2))):

        def store(at, low, high):
            out_ref[down, :, pl.ds(at, GROUP), :] = low
            out_ref[down, :, pl.ds(at + GROUP, GROUP), :] = high

        contract(mixed, kron[:, : states * bond * GROUP], store)


def project(down, row, kept_bonds, first_bond, charges, turned, summed, write):
    block = summed.shape[-1]
    for index in range(kept_bonds):
        bond_index = first_bond + index
        up = charges[bond_index, 0]
        target = down + charges[bond_index, 1]
        inside = (row + up >= 0) & (row + up < UP_VALUES) & (target >= 0) & (target < DOWN_VALUES)
        entry = jnp.where(inside, (up + 1) * DOWN_VALUES + target, ROW_SHIFTS * DOWN_VALUES)
        right = (
            summed[index * PHYS : (index + 1) * PHYS]
            .reshape(PHYS * block, block)
            .astype(jnp.bfloat16)
        )
        value = jnp.dot(turned[entry], right, preferred_element_type=jnp.float32)
        write(index, value)


def keep_part(spread, out_ref, keep_ref):
    count = keep_ref.shape[0]
    keep_ref[...] = out_ref[pl.ds(lax.axis_index("op") // spread * count, count)]


def first_kernel(chain_count, spread, bond, chunks, charges, mps_ref, turned, kron, *refs):
    env_refs, (out_ref, keep_ref, flat, deep, summed) = refs[:chunks], refs[chunks:]
    row = my_row(chain_count, spread)
    mix(env_refs, 0, mps_ref, spread, bond, flat, deep, 0, 0)
    mix(env_refs, -1, mps_ref, spread, bond, flat, deep, bond, 2 * bond)
    step = bond * GROUP
    level = jnp.concatenate([kron[:, :step], kron[:, 2 * step : 3 * step]], axis=1)
    for down, (mixed, left) in enumerate(((flat, level), (deep, kron[...]))):

        def store(at, low, high):
            summed[:, pl.ds(at, GROUP), :] = low
            summed[:, pl.ds(at + GROUP, GROUP), :] = high

        def write(index, value):
            out_ref[index, down] = value.astype(jnp.bfloat16)

        contract(mixed, left, store)
        project(down, row, bond, 0, charges, turned, summed, write)
    keep_part(spread, out_ref, keep_ref)


def main_kernel(
    chain_count, spread, bond, charges, mps_ref, turned, kron, own_ref, env_ref,
    out_ref, keep_ref, flat, deep, summed
):
    row = my_row(chain_count, spread)
    half = 2 * bond * GROUP
    mix([env_ref], -1, mps_ref, spread, bond, flat, deep, 0, 0)
    for down, (mixed, states) in enumerate(((flat, 1), (deep, 2))):

        def store(at, low, high):
            summed[:, pl.ds(at, GROUP), :] = low + own_ref[down, :, pl.ds(at, GROUP), :]
            summed[:, pl.ds(at + GROUP, GROUP), :] = (
                high + own_ref[down, :, pl.ds(at + GROUP, GROUP), :]
            )

        def write(index, value):
            out_ref[index, down] = value.astype(jnp.bfloat16)

        contract(mixed, kron[:, half : half + states * bond * GROUP], store)
        project(down, row, bond, 0, charges, turned, summed, write)
    keep_part(spread, out_ref, keep_ref)


def part_kernel(
    chain_count, spread, bond, ahead, charges, mps_ref, turned, kron, env_ref, out_ref,
    flat, deep, summed
):
    row = my_row(chain_count, spread) + ahead
    kept_bonds = out_ref.shape[0]
    rows = left_rows(bond * PHYS, kept_bonds * PHYS, spread)
    start = ahead * 2 * bond * GROUP
    first_bond = lax.axis_index("op") // spread * kept_bonds
    mix([env_ref], -ahead, mps_ref, spread, bond, flat, deep, 0, 0)
    for down, (mixed, states) in enumerate(((flat, 1), (deep, 2))):

        def store(at, low, high):
            summed[:, pl.ds(at, GROUP), :] = low
            summed[:, pl.ds(at + GROUP, GROUP), :] = high

        def write(index, value):
            out_ref[index, down] = value.astype(out_ref.dtype)

        contract(mixed, kron[rows, start : start + states * bond * GROUP], store)
        project(down, row, kept_bonds, first_bond, charges, turned, summed, write)


def sort_kernel(chain_count, spread, own_ref, before_ref, *refs):
    kept_refs, refs = refs[: chain_count - 1], refs[chain_count - 1 :]
    out_refs, result = refs[:-1], refs[-1]
    result[...] = (own_ref[...] + before_ref[...].astype(jnp.float32)).astype(jnp.bfloat16)
    chain_pos = lax.axis_index("chain")
    side = lax.rem(lax.axis_index("op"), spread)
    count = result.shape[0] // spread
    sources = list(kept_refs) + [result]
    for hop in range(chain_count):
        target_chain = jnp.bitwise_xor(chain_pos, hop)
        for turn in range(spread):
            first = jnp.bitwise_xor(side, turn) * count
            for source_site, source in enumerate(sources):
                @pl.when(target_chain == source_site)
                def _():
                    out_refs[hop * spread + turn][...] = source[pl.ds(first, count)]


def gather_kernel(chain_count, spread, *refs):
    out_ref = refs[-1]
    chain_pos = lax.axis_index("chain")
    side = lax.rem(lax.axis_index("op"), spread)
    for hop in range(chain_count):
        for turn in range(spread):
            row = place(jnp.bitwise_xor(chain_pos, hop), chain_count) * spread
            row = row + jnp.bitwise_xor(side, turn)
            out_ref[0, :, pl.ds(row * DOWN_VALUES, DOWN_VALUES)] = refs[hop * spread + turn][...]


def sweep(env_in, mps, proj, mpo, mpo_charge, block_sizes):
    chain_count = lax.axis_size("chain")
    op_count = lax.axis_size("op")
    local_bond, sectors, block, _ = env_in.shape
    bond = mpo_charge.shape[0]
    pairs = bond * PHYS
    sites = block_sizes.shape[0] - 1
    spread = UP_VALUES // chain_count
    both = ("chain", "op")
    everyone = [(c, o) for c in range(chain_count) for o in range(op_count)]
    square = (block, block)

    def flat(chain, op):
        return chain * op_count + op

    packed = call(
        functools.partial(pack_env_kernel, chain_count, spread),
        shape_of(local_bond, spread + 1, DOWN_VALUES, *square),
        [HBM],
        [env_in.reshape(local_bond, UP_VALUES, DOWN_VALUES, *square)],
        [pltpu.SemaphoreType.DMA((2 * local_bond,))],
        limit=60,
        place_out=VMEM,
    )
    own_packed = call(
        functools.partial(pack_env_kernel, chain_count, spread),
        shape_of(local_bond, spread + 1, DOWN_VALUES, *square),
        [ANY],
        [env_in.reshape(local_bond, UP_VALUES, DOWN_VALUES, *square)],
        [pltpu.SemaphoreType.DMA((2 * local_bond,))],
    )
    received = [packed]
    for hop in range(spread, op_count, spread):
        received.append(lax.ppermute(packed, "op", [(o, o ^ hop) for o in range(op_count)]))
    chunks = []
    for piece in received:
        chunks.append(piece)
        for turn in range(1, spread):
            chunks.append(lax.ppermute(piece, "op", [(o, o ^ turn) for o in range(op_count)]))
    chunks[0] = own_packed

    blocks = proj_start(None, spread)
    far = chain_count - 1
    moves = len(MPS_PARTS) + sum(part[2] for part in PROJ_PARTS)
    tensors = [mps, proj.reshape(1, PHYS, UP_VALUES, DOWN_VALUES, *square)]
    parcels = call(
        functools.partial(pack_site_kernel, chain_count, spread, 1),
        [shape_of(blocks, *square)] * far,
        [HBM, HBM],
        tensors,
        [pltpu.SemaphoreType.DMA((moves * far,))],
        limit=60,
        place_out=VMEM,
    )
    parcels = call(
        functools.partial(pack_site_kernel, chain_count, spread, 0),
        [shape_of(blocks, *square)],
        [ANY, ANY],
        tensors,
        [pltpu.SemaphoreType.DMA((moves,))],
    ) + parcels
    weights = [parcels[0]]
    for hop in range(1, far):
        weights.append(
            lax.ppermute(parcels[hop], "chain", [(c, c ^ hop) for c in range(chain_count)])
        )
    weights.append(lax.ppermute(parcels[far], "chain", [(0, far)]))
    weights.append(
        lax.ppermute(parcels[far], "chain", [(c, c ^ far) for c in range(1, chain_count)])
    )
    turned_weights = []
    for piece in weights:
        turned_weights.append(
            [piece]
            + [
                lax.ppermute(piece, "op", [(o, o ^ turn) for o in range(op_count)])
                for turn in range(1, spread)
            ]
        )
    weights = turned_weights
    matrix = mpo_matrix(mpo[0])
    matrix = jnp.pad(matrix, ((0, 0), (0, block - matrix.shape[1])))
    matrices = [matrix]
    for hop in range(1, chain_count):
        matrices.append(lax.ppermute(matrix, "chain", [(c, c ^ hop) for c in range(chain_count)]))
    extra_count = sum(part[2] for part in PROJ_PARTS)
    extras = list(call(
        functools.partial(pack_extra_kernel, chain_count, spread),
        [shape_of(extra_count, *square)] * chain_count,
        [ANY],
        tensors[1:],
        [pltpu.SemaphoreType.DMA((chain_count * len(PROJ_PARTS),))],
    ))
    middle = chain_count // 2
    for hop in range(1, chain_count):
        first_stop = far ^ (middle if hop == far else hop)
        extras[hop] = lax.ppermute(extras[hop], "chain", [(far, first_stop)])
    extras[far] = lax.ppermute(extras[far], "chain", [(far ^ middle, 0)])
    mask = call(mask_kernel, shape_of(pairs, block, dtype=jnp.float32), [SMEM], [mpo_charge])

    halo = []
    for c, o in everyone:
        at = place(c, chain_count)
        if o % spread < spread - 1:
            halo.append((flat(c, o), flat(c, o + 1)))
        elif at < chain_count - 1:
            halo.append((flat(c, o), flat(ring_chain(at + 1, chain_count), o - spread + 1)))

    keep = local_bond * spread
    kept = []
    mixed_scratch = [
        pltpu.VMEM((bond, *square), jnp.float32),
        pltpu.VMEM((2 * bond, *square), jnp.float32),
    ]
    table = shape_of(ROW_SHIFTS * DOWN_VALUES + 1, block, PHYS * block)
    full = [shape_of(bond, DOWN_VALUES, *square), shape_of(keep, DOWN_VALUES, *square)]
    for site in range(sites):
        last = site == sites - 1
        masked, turned, kron, *more = call(
            functools.partial(
                prep_kernel, site, last, chain_count, spread, bond, block, chain_count
            ),
            [
                shape_of(len(MPS_BLOCKS), *square),
                table,
                shape_of(pairs * GROUP, pairs * GROUP),
            ]
            + [table] * last,
            [SMEM, VMEM]
            + [VMEM] * chain_count
            + [ANY] * (chain_count * spread)
            + [VMEM] * (chain_count * last),
            [block_sizes, mask]
            + matrices
            + sum(weights[:far], [])
            + weights[far + 1 if site else far]
            + extras * last,
            [
                pltpu.VMEM((spread, blocks, *square), jnp.bfloat16),
                pltpu.SemaphoreType.DMA((spread,)),
            ],
        )
        if site == 0:
            finished, part = call(
                functools.partial(first_kernel, chain_count, spread, bond, len(chunks)),
                full,
                [SMEM] + [VMEM] * (3 + len(chunks)),
                [mpo_charge, masked, turned, kron] + chunks,
                [
                    pltpu.VMEM((2 * bond, *square), jnp.float32),
                    pltpu.VMEM((4 * bond, *square), jnp.float32),
                    pltpu.VMEM((pairs, *square), jnp.float32),
                ],
                limit=28,
            )
            kept.append(part)
        elif not last:
            before = lax.ppermute(finished, both, halo)
            own = call(
                functools.partial(own_kernel, spread, bond),
                shape_of(DOWN_VALUES, pairs, *square, dtype=jnp.float32),
                [VMEM] * 3,
                [masked, kron, finished],
                mixed_scratch,
            )
            finished, part = call(
                functools.partial(main_kernel, chain_count, spread, bond),
                full,
                [SMEM] + [VMEM] * 5,
                [mpo_charge, masked, turned, kron, own, before],
                mixed_scratch + [pltpu.VMEM((pairs, *square), jnp.float32)],
                limit=28,
            )
            kept.append(part)
        else:
            parts = [
                call(
                    functools.partial(part_kernel, chain_count, spread, bond, ahead),
                    shape_of(keep, DOWN_VALUES, *square, dtype=dtype),
                    [SMEM] + [VMEM] * 4,
                    [mpo_charge, masked, entries, kron, finished],
                    mixed_scratch + [pltpu.VMEM((keep * PHYS, *square), jnp.float32)],
                    limit=28,
                )
                for ahead, entries, dtype in (
                    (1, more[0], jnp.bfloat16),
                    (0, turned, jnp.float32),
                )
            ]
            before = lax.ppermute(parts[0], both, halo)
            results = call(
                functools.partial(sort_kernel, chain_count, spread),
                [shape_of(local_bond, DOWN_VALUES, *square)] * (chain_count * spread),
                [VMEM] * (2 + len(kept)),
                [parts[1], before] + kept,
                [pltpu.VMEM((keep, DOWN_VALUES, *square), jnp.bfloat16)],
            )

    arrived = []
    for hop in range(chain_count):
        for turn in range(spread):
            piece = results[hop * spread + turn]
            if hop or turn:
                piece = lax.ppermute(
                    piece, both, [(flat(c, o), flat(c ^ hop, o ^ turn)) for c, o in everyone]
                )
            arrived.append(piece)
    return call(
        functools.partial(gather_kernel, chain_count, spread),
        shape_of(1, local_bond, sectors, *square),
        [VMEM] * len(arrived),
        arrived,
    )


def solution(mesh):
    return jax.shard_map(
        sweep,
        mesh=mesh,
        in_specs=(
            P("op", None, None, None),
            P("chain", None, None, None, None),
            P("chain", None, None, None, None),
            P("chain", None, None, None, None),
            P(),
            P(),
        ),
        out_specs=P("chain", "op", None, None, None),
        check_vma=False,
    )
```

time: 154 us -> 165 us (1.071)
  the two profiles are of different devices: /device:TPU:15 before, /device:TPU:25 now
where the time goes in v2:
time: 165 us; the launch traced here: 164 us
  waiting for transfers between devices  74.1 us (45%)
  Pallas kernels  38.4 us (23%)
  starting transfers between devices  37.7 us (23%)
  local copies, waits for them, and re-layouts  12.9 us (8%)
    pallas_call x19, Pallas kernels, plain_call(): pl.pallas_call(kernel, out_shape=out_shape, in_specs=specs, out_specs=pla...  38.4 us
    ppermute x3, waiting for transfers between devices, sweep(): lax.ppermute(packed, 'op', [(o, o ^ hop) for o in range(op_count)])  22.6 us
    ppermute x3, waiting for transfers between devices, sweep(): lax.ppermute(matrix, 'chain', [(c, c ^ hop) for c in range(chain_count)])  21.7 us
    unnamed x39, local copies, waits for them, and re-layouts  11.9 us
    ppermute x1, waiting for transfers between devices, sweep(): extras[far] = lax.ppermute(extras[far], 'chain', [(far ^ middle, 0)])  10.6 us
    ppermute x7, waiting for transfers between devices, sweep(): lax.ppermute(piece, both, [(flat(c, o), flat(c ^ hop, o ^ turn)) for c, o...  10.3 us
    ppermute x2, starting transfers between devices, sweep(): before = lax.ppermute(finished, both, halo)  10.2 us
    ppermute x7, starting transfers between devices, sweep(): lax.ppermute(piece, both, [(flat(c, o), flat(c ^ hop, o ^ turn)) for c, o...  6.73 us
  transfers between devices with their start and end apart: 33, of which 12 were waited for; matrix products, arithmetic and copies ran while one was open for 2% of the time, Pallas kernels for 15%

profile of v2, /device:TPU:25, one launch (start us, length us, event | category | flops | bytes accessed | tf_op | source)
XLA Modules:
  0.0 163.6 jit_solution(14166110699794411551)
XLA Ops:
  0.0 2.9 %shard_map.66 = (bf16[18,128,128]{2,1,0:T(8,128)(2,1)}, bf16[18,128,128]{2,1,0:T(8,128)(2,1)}, bf16[18,128,128]{2,1,0:T(8,128)(2,1)}) custom-call(bf16[1,4,16,128,128]{4,3,2,1,0:T(8,128)(2,1)} %mps_ref.3, bf16[1,4,8,2,128,128]{5,4,3,2,1,0:T(8,128)(2,1)} %bitcast.5), custom_call_target="tpu_custom_call" | custom-call | flops 100000000 | bytes 1000000 | tf_op jit(solution)/shard_map/pallas_call | solution.py:77
  5.5 1.8 %shard_map.73 = bf16[2,3,2,128,128]{4,3,2,1,0:T(8,128)(2,1)} custom-call(bf16[2,8,2,128,128]{4,3,2,1,0:T(8,128)(2,1)} %bitcast.8), custom_call_target="tpu_custom_call" | custom-call | flops 100000000 | bytes 1000000 | tf_op jit(solution)/shard_map/pallas_call | solution.py:77
  7.3 2.9 %collective-permute-start.14 = (bf16[18,128,128]{2,1,0:T(8,128)(2,1)}, bf16[18,128,128]{2,1,0:T(8,128)(2,1)}, u32[]{:S(2)}, u32[]{:S(2)}) collective-permute-start(bf16[18,128,128]{2,1,0:T(8,128)(2,1)} %get-tuple-element.41), channel_id=1, source_target_pairs={{0,24},{1,25},{2,26},{3,27},{4,28},{5,29},{6,30},{7,31}} | collective-permute-start | bytes 1769480 | tf_op jit(solution)/shard_map/ppermute | solution.py:535
  11.5 18.0 %collective-permute-done.2.refs_3_ = bf16[64,128]{1,0:T(8,128)(2,1)S(1)} collective-permute-done((bf16[64,128]{1,0:T(8,128)(2,1)S(1)}, bf16[64,128]{1,0:T(8,128)(2,1)S(1)}, u32[]{:S(2)}, u32[]{:S(2)}) %collective-permute-start.2) | collective-permute-done | bytes 16416 | tf_op jit(solution)/shard_map/ppermute | solution.py:553
  29.5 2.6 %collective-permute-done.1.refs_2_ = bf16[64,128]{1,0:T(8,128)(2,1)S(1)} collective-permute-done((bf16[64,128]{1,0:T(8,128)(2,1)S(1)}, bf16[64,128]{1,0:T(8,128)(2,1)S(1)}, u32[]{:S(2)}, u32[]{:S(2)}) %collective-permute-start.1) | collective-permute-done | bytes 16416 | tf_op jit(solution)/shard_map/ppermute | solution.py:553
  32.1 2.0 %collective-permute-start = (bf16[64,128]{1,0:T(8,128)(2,1)S(1)}, bf16[64,128]{1,0:T(8,128)(2,1)S(1)}, u32[]{:S(2)}, u32[]{:S(2)}) collective-permute-start(bf16[64,128]{1,0:T(8,128)(2,1)S(1)} %pad.4.refs_0_), channel_id=1, source_target_pairs={{0,8},{8,0},{16,24},{24,16},{1,9},{9,1},{17,25},{25,17},{2,10},{10... | collective-permute-start | bytes 49160 | tf_op jit(solution)/shard_map/ppermute | solution.py:553
  35.3 1.6 copy-done
  36.9 1.6 copy-done.2
  39.1 3.6 %collective-permute-start.3 = (bf16[18,128,128]{2,1,0:T(8,128)(2,1)S(1)}, bf16[18,128,128]{2,1,0:T(8,128)(2,1)S(1)}, u32[]{:S(2)}, u32[]{:S(2)}) collective-permute-start(bf16[18,128,128]{2,1,0:T(8,128)(2,1)S(1)} %shard_map.65.refs_4_), channel_id=1, source_target_pairs={{0,1},{1,0},{2,3},{3,2},{4,5},{5,4},{6,7},{7,6},{8,9},{9,8},{10,11... | collective-permute-start | bytes 1769480 | tf_op jit(solution)/shard_map/ppermute | solution.py:544
  43.2 12.6 %collective-permute-done.19.refs_4_ = bf16[2,3,2,128,128]{4,3,2,1,0:T(8,128)(2,1)} collective-permute-done((bf16[2,3,2,128,128]{4,3,2,1,0:T(8,128)(2,1)}, bf16[2,3,2,128,128]{4,3,2,1,0:T(8,128)(2,1)}, u32[]{:S(2)}, u32[]{:S(2)}) %collective-permute-start.19) | collective-permute-done | bytes 393248 | tf_op jit(solution)/shard_map/ppermute | solution.py:502
  56.3 10.0 %collective-permute-done.17.refs_2_ = bf16[2,3,2,128,128]{4,3,2,1,0:T(8,128)(2,1)} collective-permute-done((bf16[2,3,2,128,128]{4,3,2,1,0:T(8,128)(2,1)}, bf16[2,3,2,128,128]{4,3,2,1,0:T(8,128)(2,1)}, u32[]{:S(2)}, u32[]{:S(2)}) %collective-permute-start.17) | collective-permute-done | bytes 393248 | tf_op jit(solution)/shard_map/ppermute | solution.py:502
  78.8 1.4 shard_map.71
  80.9 5.8 %shard_map.74 = (bf16[16,2,128,128]{3,2,1,0:T(8,128)(2,1)S(1)}, bf16[4,2,128,128]{3,2,1,0:T(8,128)(2,1)S(1)}) custom-call(s32[16,2]{1,0:T(8,128)S(1)} %copy-done.7, bf16[6,128,128]{2,1,0:T(8,128)(2,1)S(1)} %get-tuple-element.55.mps_ref, bf16[7,128,512]{2,1,0:T(8,128)(2,1)S(1)} %get-tuple-element.56.turned, bf16[512,512]{1,0:T(8,128)(2,1)S(1)} %get-tuple-element.57.kron, ...), custom_call_target="tpu_custom_call" | custom-call | flops 100000000 | bytes 1000000 | tf_op jit(solution)/shard_map/pallas_call | solution.py:77
  86.8 5.8 %collective-permute-start.23 = (bf16[16,2,128,128]{3,2,1,0:T(8,128)(2,1)S(1)}, bf16[16,2,128,128]{3,2,1,0:T(8,128)(2,1)S(1)}, u32[]{:S(2)}, u32[]{:S(2)}) collective-permute-start(bf16[16,2,128,128]{3,2,1,0:T(8,128)(2,1)S(1)} %get-tuple-element.58.env_ref), channel_id=1, source_target_pairs={{0,1},{1,8},{2,3},{3,10},{4,5},{5,12},{6,7},{7,14},{8,9},{9,24},{1... | collective-permute-start | bytes 3145736 | tf_op jit(solution)/shard_map/ppermute | solution.py:626
  92.6 2.2 %collective-permute-done.9.refs_11_ = bf16[18,128,128]{2,1,0:T(8,128)(2,1)S(1)} collective-permute-done((bf16[18,128,128]{2,1,0:T(8,128)(2,1)}, bf16[18,128,128]{2,1,0:T(8,128)(2,1)S(1)}, u32[]{:S(2)}, u32[]{:S(2)}) %collective-permute-start.9) | collective-permute-done | bytes 589856 | tf_op jit(solution)/shard_map/ppermute | solution.py:544
  94.9 1.5 shard_map.70
  96.4 2.0 %shard_map.75.own_ref = f32[2,64,128,128]{3,2,1,0:T(8,128)S(1)} custom-call(bf16[6,128,128]{2,1,0:T(8,128)(2,1)S(1)} %get-tuple-element.52.mps_ref, bf16[512,512]{1,0:T(8,128)(2,1)S(1)} %get-tuple-element.54.kron, bf16[16,2,128,128]{3,2,1,0:T(8,128)(2,1)S(1)} %get-tuple-element.58.env_ref), custom_call_target="tpu_custom_call" | custom-call | flops 100000000 | bytes 1000000 | tf_op jit(solution)/shard_map/pallas_call | solution.py:77
  98.5 5.8 %collective-permute-done.23.env_ref = bf16[16,2,128,128]{3,2,1,0:T(8,128)(2,1)S(1)} collective-permute-done((bf16[16,2,128,128]{3,2,1,0:T(8,128)(2,1)S(1)}, bf16[16,2,128,128]{3,2,1,0:T(8,128)(2,1)S(1)}, u32[]{:S(2)}, u32[]{:S(2)}) %collective-permute-start.23) | collective-permute-done | bytes 1048608 | tf_op jit(solution)/shard_map/ppermute | solution.py:626
  104.3 4.0 %shard_map.76 = (bf16[16,2,128,128]{3,2,1,0:T(8,128)(2,1)S(1)}, bf16[4,2,128,128]{3,2,1,0:T(8,128)(2,1)S(1)}) custom-call(s32[16,2]{1,0:T(8,128)S(1)} %copy-done.7, bf16[6,128,128]{2,1,0:T(8,128)(2,1)S(1)} %get-tuple-element.52.mps_ref, bf16[7,128,512]{2,1,0:T(8,128)(2,1)S(1)} %get-tuple-element.53.turned, bf16[512,512]{1,0:T(8,128)(2,1)S(1)} %get-tuple-element.54.kron, ...), custom_call_target="tpu_custom_call" | custom-call | flops 100000000 | bytes 1000000 | tf_op jit(solution)/shard_map/pallas_call | solution.py:77
  108.3 4.4 %collective-permute-start.24 = (bf16[16,2,128,128]{3,2,1,0:T(8,128)(2,1)S(1)}, bf16[16,2,128,128]{3,2,1,0:T(8,128)(2,1)S(1)}, u32[]{:S(2)}, u32[]{:S(2)}) collective-permute-start(bf16[16,2,128,128]{3,2,1,0:T(8,128)(2,1)S(1)} %get-tuple-element.59.env_ref), channel_id=1, source_target_pairs={{0,1},{1,8},{2,3},{3,10},{4,5},{5,12},{6,7},{7,14},{8,9},{9,24},{1... | collective-permute-start | bytes 3145736 | tf_op jit(solution)/shard_map/ppermute | solution.py:626
  117.3 1.4 shard_map.69
  118.7 10.6 %collective-permute-done.13.refs_15_ = bf16[6,128,128]{2,1,0:T(8,128)(2,1)S(1)} collective-permute-done((bf16[6,128,128]{2,1,0:T(8,128)(2,1)S(1)}, bf16[6,128,128]{2,1,0:T(8,128)(2,1)S(1)}, u32[]{:S(2)}, u32[]{:S(2)}) %collective-permute-start.13) | collective-permute-done | bytes 196640 | tf_op jit(solution)/shard_map/ppermute | solution.py:566
  129.3 2.4 %shard_map.68 = (bf16[6,128,128]{2,1,0:T(8,128)(2,1)S(1)}, bf16[7,128,512]{2,1,0:T(8,128)(2,1)S(1)}, bf16[512,512]{1,0:T(8,128)(2,1)S(1)}, bf16[7,128,512]{2,1,0:T(8,128)(2,1)S(1)}) custom-call(s32[5,16]{1,0:T(8,128)S(1)} %copy-done.18, f32[64,128]{1,0:T(8,128)S(1)} %shard_map.64.mask, bf16[64,128]{1,0:T(8,128)(2,1)S(1)} %pad.4.refs_0_, ...), custom_call_target="tpu_custom_call" | custom-call | flops 100000000 | bytes 1000000 | tf_op jit(solution)/shard_map/pallas_call | solution.py:77
  131.7 2.0 %shard_map.77.own_ref = f32[2,64,128,128]{3,2,1,0:T(8,128)S(1)} custom-call(bf16[6,128,128]{2,1,0:T(8,128)(2,1)S(1)} %get-tuple-element.49.mps_ref, bf16[512,512]{1,0:T(8,128)(2,1)S(1)} %get-tuple-element.51.kron, bf16[16,2,128,128]{3,2,1,0:T(8,128)(2,1)S(1)} %get-tuple-element.59.env_ref), custom_call_target="tpu_custom_call" | custom-call | flops 100000000 | bytes 1000000 | tf_op jit(solution)/shard_map/pallas_call | solution.py:77
  133.7 4.0 %shard_map.78 = (bf16[16,2,128,128]{3,2,1,0:T(8,128)(2,1)S(1)}, bf16[4,2,128,128]{3,2,1,0:T(8,128)(2,1)S(1)}) custom-call(s32[16,2]{1,0:T(8,128)S(1)} %copy-done.7, bf16[6,128,128]{2,1,0:T(8,128)(2,1)S(1)} %get-tuple-element.49.mps_ref, bf16[7,128,512]{2,1,0:T(8,128)(2,1)S(1)} %get-tuple-element.50.turned, bf16[512,512]{1,0:T(8,128)(2,1)S(1)} %get-tuple-element.51.kron, ...), custom_call_target="tpu_custom_call" | custom-call | flops 100000000 | bytes 1000000 | tf_op jit(solution)/shard_map/pallas_call | solution.py:77
  137.7 2.4 %shard_map.80 = bf16[4,2,128,128]{3,2,1,0:T(8,128)(2,1)S(1)} custom-call(s32[16,2]{1,0:T(8,128)S(1)} %copy-done.7, bf16[6,128,128]{2,1,0:T(8,128)(2,1)S(1)} %get-tuple-element.46.mps_ref, bf16[7,128,512]{2,1,0:T(8,128)(2,1)S(1)} %get-tuple-element.61.turned, bf16[512,512]{1,0:T(8,128)(2,1)S(1)} %get-tuple-element.48.kron, ...), custom_call_target="tpu_custom_call" | custom-call | flops 100000000 | bytes 1000000 | tf_op jit(solution)/shard_map/pallas_call | solution.py:77
  140.1 1.9 %collective-permute-start.25 = (bf16[4,2,128,128]{3,2,1,0:T(8,128)(2,1)S(1)}, bf16[4,2,128,128]{3,2,1,0:T(8,128)(2,1)S(1)}, u32[]{:S(2)}, u32[]{:S(2)}) collective-permute-start(bf16[4,2,128,128]{3,2,1,0:T(8,128)(2,1)S(1)} %shard_map.80), channel_id=1, source_target_pairs={{0,1},{1,8},{2,3},{3,10},{4,5},{5,12},{6,7},{7,14},{8,9},{9,24},{1... | collective-permute-start | bytes 786440 | tf_op jit(solution)/shard_map/ppermute | solution.py:658
  142.0 2.4 %shard_map.79.own_ref = f32[4,2,128,128]{3,2,1,0:T(8,128)S(1)} custom-call(s32[16,2]{1,0:T(8,128)S(1)} %copy-done.7, bf16[6,128,128]{2,1,0:T(8,128)(2,1)S(1)} %get-tuple-element.46.mps_ref, bf16[7,128,512]{2,1,0:T(8,128)(2,1)S(1)} %get-tuple-element.47.turned, bf16[512,512]{1,0:T(8,128)(2,1)S(1)} %get-tuple-element.48.kron, ...), custom_call_target="tpu_custom_call" | custom-call | flops 100000000 | bytes 1000000 | tf_op jit(solution)/shard_map/pallas_call | solution.py:77
  145.6 1.7 %collective-permute-start.26 = (bf16[2,2,128,128]{3,2,1,0:T(8,128)(2,1)S(1)}, bf16[2,2,128,128]{3,2,1,0:T(8,128)(2,1)S(1)}, u32[]{:S(2)}, u32[]{:S(2)}) collective-permute-start(bf16[2,2,128,128]{3,2,1,0:T(8,128)(2,1)S(1)} %get-tuple-element.66), channel_id=1, source_target_pairs={{0,1},{1,0},{2,3},{3,2},{4,5},{5,4},{6,7},{7,6},{8,9},{9,8},{10,11... | collective-permute-start | bytes 393224 | tf_op jit(solution)/shard_map/ppermute | solution.py:672
  148.9 1.8 %collective-permute-start.30 = (bf16[2,2,128,128]{3,2,1,0:T(8,128)(2,1)S(1)}, bf16[2,2,128,128]{3,2,1,0:T(8,128)(2,1)S(1)}, u32[]{:S(2)}, u32[]{:S(2)}) collective-permute-start(bf16[2,2,128,128]{3,2,1,0:T(8,128)(2,1)S(1)} %get-tuple-element.70), channel_id=1, source_target_pairs={{0,17},{1,16},{2,19},{3,18},{4,21},{5,20},{6,23},{7,22},{8,25},{9,... | collective-permute-start | bytes 393224 | tf_op jit(solution)/shard_map/ppermute | solution.py:672
  153.3 2.8 %collective-permute-done.28.refs_3_ = bf16[2,2,128,128]{3,2,1,0:T(8,128)(2,1)S(1)} collective-permute-done((bf16[2,2,128,128]{3,2,1,0:T(8,128)(2,1)S(1)}, bf16[2,2,128,128]{3,2,1,0:T(8,128)(2,1)S(1)}, u32[]{:S(2)}, u32[]{:S(2)}) %collective-permute-start.28) | collective-permute-done | bytes 131104 | tf_op jit(solution)/shard_map/ppermute | solution.py:672
  156.1 6.5 %collective-permute-done.30.refs_5_ = bf16[2,2,128,128]{3,2,1,0:T(8,128)(2,1)S(1)} collective-permute-done((bf16[2,2,128,128]{3,2,1,0:T(8,128)(2,1)S(1)}, bf16[2,2,128,128]{3,2,1,0:T(8,128)(2,1)S(1)}, u32[]{:S(2)}, u32[]{:S(2)}) %collective-permute-start.30) | collective-permute-done | bytes 131104 | tf_op jit(solution)/shard_map/ppermute | solution.py:672
  (97 shorter events, 30.9 us)
Async XLA Ops:
  2.9 39.8 %collective-permute-start.4 = (bf16[18,128,128]{2,1,0:T(8,128)(2,1)}, bf16[18,128,128]{2,1,0:T(8,128)(2,1)S(1)}, u32[]{:S(2)}, u32[]{:S(2)}) collective-permute-start(bf16[18,128,128]{2,1,0:T(8,128)(2,1)} %get-tuple-element.39), channel_id=1, source_target_pairs={{0,8},{8,0},{16,24},{24,16},{1,9},{9,1},{17,25},{25,17},{2,10},{10... | collective-permute-start | bytes 1769480 | tf_op jit(solution)/shard_map/ppermute | solution.py:533
  4.2 38.6 %collective-permute-start.6 = (bf16[18,128,128]{2,1,0:T(8,128)(2,1)}, bf16[18,128,128]{2,1,0:T(8,128)(2,1)S(1)}, u32[]{:S(2)}, u32[]{:S(2)}) collective-permute-start(bf16[18,128,128]{2,1,0:T(8,128)(2,1)} %get-tuple-element.40), channel_id=1, source_target_pairs={{0,16},{8,24},{16,0},{24,8},{1,17},{9,25},{17,1},{25,9},{2,18},{10... | collective-permute-start | bytes 1769480 | tf_op jit(solution)/shard_map/ppermute | solution.py:533
  7.3 31.8 %collective-permute-start.21 = (bf16[2,3,2,128,128]{4,3,2,1,0:T(8,128)(2,1)}, bf16[2,3,2,128,128]{4,3,2,1,0:T(8,128)(2,1)}, u32[]{:S(2)}, u32[]{:S(2)}) collective-permute-start(bf16[2,3,2,128,128]{4,3,2,1,0:T(8,128)(2,1)} %shard_map.73), channel_id=1, source_target_pairs={{0,6},{1,7},{2,4},{3,5},{4,2},{5,3},{6,0},{7,1},{8,14},{9,15},{10,... | collective-permute-start | bytes 1179656 | tf_op jit(solution)/shard_map/ppermute | solution.py:502
  7.3 48.4 %collective-permute-start.14 = (bf16[18,128,128]{2,1,0:T(8,128)(2,1)}, bf16[18,128,128]{2,1,0:T(8,128)(2,1)}, u32[]{:S(2)}, u32[]{:S(2)}) collective-permute-start(bf16[18,128,128]{2,1,0:T(8,128)(2,1)} %get-tuple-element.41), channel_id=1, source_target_pairs={{0,24},{1,25},{2,26},{3,27},{4,28},{5,29},{6,30},{7,31}} | collective-permute-start | bytes 1769480 | tf_op jit(solution)/shard_map/ppermute | solution.py:535
  11.4 18.0 %collective-permute-start.2 = (bf16[64,128]{1,0:T(8,128)(2,1)S(1)}, bf16[64,128]{1,0:T(8,128)(2,1)S(1)}, u32[]{:S(2)}, u32[]{:S(2)}) collective-permute-start(bf16[64,128]{1,0:T(8,128)(2,1)S(1)} %pad.4.refs_0_), channel_id=1, source_target_pairs={{0,24},{8,16},{16,8},{24,0},{1,25},{9,17},{17,9},{25,1},{2,26},{10... | collective-permute-start | bytes 49160 | tf_op jit(solution)/shard_map/ppermute | solution.py:553
  29.5 2.6 %collective-permute-start.1 = (bf16[64,128]{1,0:T(8,128)(2,1)S(1)}, bf16[64,128]{1,0:T(8,128)(2,1)S(1)}, u32[]{:S(2)}, u32[]{:S(2)}) collective-permute-start(bf16[64,128]{1,0:T(8,128)(2,1)S(1)} %pad.4.refs_0_), channel_id=1, source_target_pairs={{0,16},{8,24},{16,0},{24,8},{1,17},{9,25},{17,1},{25,9},{2,18},{10... | collective-permute-start | bytes 49160 | tf_op jit(solution)/shard_map/ppermute | solution.py:553
  32.1 3.2 %collective-permute-start = (bf16[64,128]{1,0:T(8,128)(2,1)S(1)}, bf16[64,128]{1,0:T(8,128)(2,1)S(1)}, u32[]{:S(2)}, u32[]{:S(2)}) collective-permute-start(bf16[64,128]{1,0:T(8,128)(2,1)S(1)} %pad.4.refs_0_), channel_id=1, source_target_pairs={{0,8},{8,0},{16,24},{24,16},{1,9},{9,1},{17,25},{25,17},{2,10},{10... | collective-permute-start | bytes 49160 | tf_op jit(solution)/shard_map/ppermute | solution.py:553
  35.2 20.6 %collective-permute-start.19 = (bf16[2,3,2,128,128]{4,3,2,1,0:T(8,128)(2,1)}, bf16[2,3,2,128,128]{4,3,2,1,0:T(8,128)(2,1)}, u32[]{:S(2)}, u32[]{:S(2)}) collective-permute-start(bf16[2,3,2,128,128]{4,3,2,1,0:T(8,128)(2,1)} %shard_map.73), channel_id=1, source_target_pairs={{0,4},{1,5},{2,6},{3,7},{4,0},{5,1},{6,2},{7,3},{8,12},{9,13},{10,... | collective-permute-start | bytes 1179656 | tf_op jit(solution)/shard_map/ppermute | solution.py:502
  39.1 28.5 %collective-permute-start.3 = (bf16[18,128,128]{2,1,0:T(8,128)(2,1)S(1)}, bf16[18,128,128]{2,1,0:T(8,128)(2,1)S(1)}, u32[]{:S(2)}, u32[]{:S(2)}) collective-permute-start(bf16[18,128,128]{2,1,0:T(8,128)(2,1)S(1)} %shard_map.65.refs_4_), channel_id=1, source_target_pairs={{0,1},{1,0},{2,3},{3,2},{4,5},{5,4},{6,7},{7,6},{8,9},{9,8},{10,11... | collective-permute-start | bytes 1769480 | tf_op jit(solution)/shard_map/ppermute | solution.py:544
  42.7 24.9 %collective-permute-start.5 = (bf16[18,128,128]{2,1,0:T(8,128)(2,1)S(1)}, bf16[18,128,128]{2,1,0:T(8,128)(2,1)S(1)}, u32[]{:S(2)}, u32[]{:S(2)}) collective-permute-start(bf16[18,128,128]{2,1,0:T(8,128)(2,1)S(1)} %collective-permute-done.4.refs_6_), channel_id=1, source_target_pairs={{0,1},{1,0},{2,3},{3,2},{4,5},{5,4},{6,7},{7,6},{8,9},{9,8},{10,11... | collective-permute-start | bytes 1769480 | tf_op jit(solution)/shard_map/ppermute | solution.py:544
  42.8 25.4 %collective-permute-start.7 = (bf16[18,128,128]{2,1,0:T(8,128)(2,1)S(1)}, bf16[18,128,128]{2,1,0:T(8,128)(2,1)S(1)}, u32[]{:S(2)}, u32[]{:S(2)}) collective-permute-start(bf16[18,128,128]{2,1,0:T(8,128)(2,1)S(1)} %collective-permute-done.6.refs_8_), channel_id=1, source_target_pairs={{0,1},{1,0},{2,3},{3,2},{4,5},{5,4},{6,7},{7,6},{8,9},{9,8},{10,11... | collective-permute-start | bytes 1769480 | tf_op jit(solution)/shard_map/ppermute | solution.py:544
  55.8 10.5 %collective-permute-start.17 = (bf16[2,3,2,128,128]{4,3,2,1,0:T(8,128)(2,1)}, bf16[2,3,2,128,128]{4,3,2,1,0:T(8,128)(2,1)}, u32[]{:S(2)}, u32[]{:S(2)}) collective-permute-start(bf16[2,3,2,128,128]{4,3,2,1,0:T(8,128)(2,1)} %shard_map.73), channel_id=1, source_target_pairs={{0,2},{1,3},{2,0},{3,1},{4,6},{5,7},{6,4},{7,5},{8,10},{9,11},{10,... | collective-permute-start | bytes 1179656 | tf_op jit(solution)/shard_map/ppermute | solution.py:502
  55.8 12.4 %collective-permute-start.15 = (bf16[18,128,128]{2,1,0:T(8,128)(2,1)}, bf16[18,128,128]{2,1,0:T(8,128)(2,1)S(1)}, u32[]{:S(2)}, u32[]{:S(2)}) collective-permute-start(bf16[18,128,128]{2,1,0:T(8,128)(2,1)} %collective-permute-done.14.refs_10_), channel_id=1, source_target_pairs={{0,1},{1,0},{2,3},{3,2},{4,5},{5,4},{6,7},{7,6},{8,9},{9,8},{10,11... | collective-permute-start | bytes 1769480 | tf_op jit(solution)/shard_map/ppermute | solution.py:544
  66.3 13.9 %collective-permute-start.16 = (bf16[2,3,2,128,128]{4,3,2,1,0:T(8,128)(2,1)}, bf16[2,3,2,128,128]{4,3,2,1,0:T(8,128)(2,1)}, u32[]{:S(2)}, u32[]{:S(2)}) collective-permute-start(bf16[2,3,2,128,128]{4,3,2,1,0:T(8,128)(2,1)} %shard_map.73), channel_id=1, source_target_pairs={{0,1},{1,0},{2,3},{3,2},{4,5},{5,4},{6,7},{7,6},{8,9},{9,8},{10,11... | collective-permute-start | bytes 1179656 | tf_op jit(solution)/shard_map/ppermute | solution.py:507
  67.6 12.6 %collective-permute-start.22 = (bf16[2,3,2,128,128]{4,3,2,1,0:T(8,128)(2,1)}, bf16[2,3,2,128,128]{4,3,2,1,0:T(8,128)(2,1)}, u32[]{:S(2)}, u32[]{:S(2)}) collective-permute-start(bf16[2,3,2,128,128]{4,3,2,1,0:T(8,128)(2,1)} %collective-permute-done.21.refs_6_), channel_id=1, source_target_pairs={{0,1},{1,0},{2,3},{3,2},{4,5},{5,4},{6,7},{7,6},{8,9},{9,8},{10,11... | collective-permute-start | bytes 1179656 | tf_op jit(solution)/shard_map/ppermute | solution.py:507
  67.6 12.6 %collective-permute-start.20 = (bf16[2,3,2,128,128]{4,3,2,1,0:T(8,128)(2,1)}, bf16[2,3,2,128,128]{4,3,2,1,0:T(8,128)(2,1)}, u32[]{:S(2)}, u32[]{:S(2)}) collective-permute-start(bf16[2,3,2,128,128]{4,3,2,1,0:T(8,128)(2,1)} %collective-permute-done.19.refs_4_), channel_id=1, source_target_pairs={{0,1},{1,0},{2,3},{3,2},{4,5},{5,4},{6,7},{7,6},{8,9},{9,8},{10,11... | collective-permute-start | bytes 1179656 | tf_op jit(solution)/shard_map/ppermute | solution.py:507
  68.2 12.1 %collective-permute-start.18 = (bf16[2,3,2,128,128]{4,3,2,1,0:T(8,128)(2,1)}, bf16[2,3,2,128,128]{4,3,2,1,0:T(8,128)(2,1)}, u32[]{:S(2)}, u32[]{:S(2)}) collective-permute-start(bf16[2,3,2,128,128]{4,3,2,1,0:T(8,128)(2,1)} %collective-permute-done.17.refs_2_), channel_id=1, source_target_pairs={{0,1},{1,0},{2,3},{3,2},{4,5},{5,4},{6,7},{7,6},{8,9},{9,8},{10,11... | collective-permute-start | bytes 1179656 | tf_op jit(solution)/shard_map/ppermute | solution.py:507
  69.0 23.5 %collective-permute-start.8 = (bf16[18,128,128]{2,1,0:T(8,128)(2,1)}, bf16[18,128,128]{2,1,0:T(8,128)(2,1)}, u32[]{:S(2)}, u32[]{:S(2)}) collective-permute-start(bf16[18,128,128]{2,1,0:T(8,128)(2,1)} %get-tuple-element.41), channel_id=1, source_target_pairs={{8,16},{16,8},{24,0},{9,17},{17,9},{25,1},{10,18},{18,10},{26,2},{... | collective-permute-start | bytes 1769480 | tf_op jit(solution)/shard_map/ppermute | solution.py:537
  86.8 17.5 %collective-permute-start.23 = (bf16[16,2,128,128]{3,2,1,0:T(8,128)(2,1)S(1)}, bf16[16,2,128,128]{3,2,1,0:T(8,128)(2,1)S(1)}, u32[]{:S(2)}, u32[]{:S(2)}) collective-permute-start(bf16[16,2,128,128]{3,2,1,0:T(8,128)(2,1)S(1)} %get-tuple-element.58.env_ref), channel_id=1, source_target_pairs={{0,1},{1,8},{2,3},{3,10},{4,5},{5,12},{6,7},{7,14},{8,9},{9,24},{1... | collective-permute-start | bytes 3145736 | tf_op jit(solution)/shard_map/ppermute | solution.py:626
  92.6 2.3 %collective-permute-start.9 = (bf16[18,128,128]{2,1,0:T(8,128)(2,1)}, bf16[18,128,128]{2,1,0:T(8,128)(2,1)S(1)}, u32[]{:S(2)}, u32[]{:S(2)}) collective-permute-start(bf16[18,128,128]{2,1,0:T(8,128)(2,1)} %collective-permute-done.8.refs_10_), channel_id=1, source_target_pairs={{0,1},{1,0},{2,3},{3,2},{4,5},{5,4},{6,7},{7,6},{8,9},{9,8},{10,11... | collective-permute-start | bytes 1769480 | tf_op jit(solution)/shard_map/ppermute | solution.py:544
  108.3 25.4 %collective-permute-start.24 = (bf16[16,2,128,128]{3,2,1,0:T(8,128)(2,1)S(1)}, bf16[16,2,128,128]{3,2,1,0:T(8,128)(2,1)S(1)}, u32[]{:S(2)}, u32[]{:S(2)}) collective-permute-start(bf16[16,2,128,128]{3,2,1,0:T(8,128)(2,1)S(1)} %get-tuple-element.59.env_ref), channel_id=1, source_target_pairs={{0,1},{1,8},{2,3},{3,10},{4,5},{5,12},{6,7},{7,14},{8,9},{9,24},{1... | collective-permute-start | bytes 3145736 | tf_op jit(solution)/shard_map/ppermute | solution.py:626
  114.6 4.0 %collective-permute-start.10 = (bf16[6,128,128]{2,1,0:T(8,128)(2,1)S(1)}, bf16[6,128,128]{2,1,0:T(8,128)(2,1)S(1)}, u32[]{:S(2)}, u32[]{:S(2)}) collective-permute-start(bf16[6,128,128]{2,1,0:T(8,128)(2,1)S(1)} %get-tuple-element.43), channel_id=1, source_target_pairs={{24,16},{25,17},{26,18},{27,19},{28,20},{29,21},{30,22},{31,23}} | collective-permute-start | bytes 589832 | tf_op jit(solution)/shard_map/ppermute | solution.py:565
  115.3 3.4 %collective-permute-start.11 = (bf16[6,128,128]{2,1,0:T(8,128)(2,1)S(1)}, bf16[6,128,128]{2,1,0:T(8,128)(2,1)S(1)}, u32[]{:S(2)}, u32[]{:S(2)}) collective-permute-start(bf16[6,128,128]{2,1,0:T(8,128)(2,1)S(1)} %get-tuple-element.44), channel_id=1, source_target_pairs={{24,8},{25,9},{26,10},{27,11},{28,12},{29,13},{30,14},{31,15}} | collective-permute-start | bytes 589832 | tf_op jit(solution)/shard_map/ppermute | solution.py:565
  116.0 13.3 %collective-permute-start.13 = (bf16[6,128,128]{2,1,0:T(8,128)(2,1)S(1)}, bf16[6,128,128]{2,1,0:T(8,128)(2,1)S(1)}, u32[]{:S(2)}, u32[]{:S(2)}) collective-permute-start(bf16[6,128,128]{2,1,0:T(8,128)(2,1)S(1)} %collective-permute-done.12), channel_id=1, source_target_pairs={{8,0},{9,1},{10,2},{11,3},{12,4},{13,5},{14,6},{15,7}} | collective-permute-start | bytes 589832 | tf_op jit(solution)/shard_map/ppermute | solution.py:566
  140.1 5.2 %collective-permute-start.25 = (bf16[4,2,128,128]{3,2,1,0:T(8,128)(2,1)S(1)}, bf16[4,2,128,128]{3,2,1,0:T(8,128)(2,1)S(1)}, u32[]{:S(2)}, u32[]{:S(2)}) collective-permute-start(bf16[4,2,128,128]{3,2,1,0:T(8,128)(2,1)S(1)} %shard_map.80), channel_id=1, source_target_pairs={{0,1},{1,8},{2,3},{3,10},{4,5},{5,12},{6,7},{7,14},{8,9},{9,24},{1... | collective-permute-start | bytes 786440 | tf_op jit(solution)/shard_map/ppermute | solution.py:658
  145.6 5.2 %collective-permute-start.26 = (bf16[2,2,128,128]{3,2,1,0:T(8,128)(2,1)S(1)}, bf16[2,2,128,128]{3,2,1,0:T(8,128)(2,1)S(1)}, u32[]{:S(2)}, u32[]{:S(2)}) collective-permute-start(bf16[2,2,128,128]{3,2,1,0:T(8,128)(2,1)S(1)} %get-tuple-element.66), channel_id=1, source_target_pairs={{0,1},{1,0},{2,3},{3,2},{4,5},{5,4},{6,7},{7,6},{8,9},{9,8},{10,11... | collective-permute-start | bytes 393224 | tf_op jit(solution)/shard_map/ppermute | solution.py:672
  147.2 5.0 %collective-permute-start.27 = (bf16[2,2,128,128]{3,2,1,0:T(8,128)(2,1)S(1)}, bf16[2,2,128,128]{3,2,1,0:T(8,128)(2,1)S(1)}, u32[]{:S(2)}, u32[]{:S(2)}) collective-permute-start(bf16[2,2,128,128]{3,2,1,0:T(8,128)(2,1)S(1)} %get-tuple-element.67), channel_id=1, source_target_pairs={{0,8},{1,9},{2,10},{3,11},{4,12},{5,13},{6,14},{7,15},{8,0},{9,1},... | collective-permute-start | bytes 393224 | tf_op jit(solution)/shard_map/ppermute | solution.py:672
  148.2 7.9 %collective-permute-start.28 = (bf16[2,2,128,128]{3,2,1,0:T(8,128)(2,1)S(1)}, bf16[2,2,128,128]{3,2,1,0:T(8,128)(2,1)S(1)}, u32[]{:S(2)}, u32[]{:S(2)}) collective-permute-start(bf16[2,2,128,128]{3,2,1,0:T(8,128)(2,1)S(1)} %get-tuple-element.68), channel_id=1, source_target_pairs={{0,9},{1,8},{2,11},{3,10},{4,13},{5,12},{6,15},{7,14},{8,1},{9,0},... | collective-permute-start | bytes 393224 | tf_op jit(solution)/shard_map/ppermute | solution.py:672
  148.9 7.2 %collective-permute-start.29 = (bf16[2,2,128,128]{3,2,1,0:T(8,128)(2,1)S(1)}, bf16[2,2,128,128]{3,2,1,0:T(8,128)(2,1)S(1)}, u32[]{:S(2)}, u32[]{:S(2)}) collective-permute-start(bf16[2,2,128,128]{3,2,1,0:T(8,128)(2,1)S(1)} %get-tuple-element.69), channel_id=1, source_target_pairs={{0,16},{1,17},{2,18},{3,19},{4,20},{5,21},{6,22},{7,23},{8,24},{9,... | collective-permute-start | bytes 393224 | tf_op jit(solution)/shard_map/ppermute | solution.py:672
  148.9 13.6 %collective-permute-start.30 = (bf16[2,2,128,128]{3,2,1,0:T(8,128)(2,1)S(1)}, bf16[2,2,128,128]{3,2,1,0:T(8,128)(2,1)S(1)}, u32[]{:S(2)}, u32[]{:S(2)}) collective-permute-start(bf16[2,2,128,128]{3,2,1,0:T(8,128)(2,1)S(1)} %get-tuple-element.70), channel_id=1, source_target_pairs={{0,17},{1,16},{2,19},{3,18},{4,21},{5,20},{6,23},{7,22},{8,25},{9,... | collective-permute-start | bytes 393224 | tf_op jit(solution)/shard_map/ppermute | solution.py:672
  150.7 11.9 %collective-permute-start.31 = (bf16[2,2,128,128]{3,2,1,0:T(8,128)(2,1)S(1)}, bf16[2,2,128,128]{3,2,1,0:T(8,128)(2,1)S(1)}, u32[]{:S(2)}, u32[]{:S(2)}) collective-permute-start(bf16[2,2,128,128]{3,2,1,0:T(8,128)(2,1)S(1)} %get-tuple-element.71), channel_id=1, source_target_pairs={{0,24},{1,25},{2,26},{3,27},{4,28},{5,29},{6,30},{7,31},{8,16},{9,... | collective-permute-start | bytes 393224 | tf_op jit(solution)/shard_map/ppermute | solution.py:672
  152.2 10.4 %collective-permute-start.32 = (bf16[2,2,128,128]{3,2,1,0:T(8,128)(2,1)S(1)}, bf16[2,2,128,128]{3,2,1,0:T(8,128)(2,1)S(1)}, u32[]{:S(2)}, u32[]{:S(2)}) collective-permute-start(bf16[2,2,128,128]{3,2,1,0:T(8,128)(2,1)S(1)} %get-tuple-element.72), channel_id=1, source_target_pairs={{0,25},{1,24},{2,27},{3,26},{4,29},{5,28},{6,31},{7,30},{8,17},{9,... | collective-permute-start | bytes 393224 | tf_op jit(solution)/shard_map/ppermute | solution.py:672
  (20 other events, 137.0 us)
